TPU v7x, 256 devices: a whole 4x4x8 slice. The times are simulated.
256 devices in a mesh: dp: 8 (over y, core), space: 32 (over z, x).
Axes of the slice: x: 4, y: 4, z: 8, core: 2. Of those that a mesh axis runs over, the one named last changes fastest.
Arguments:
- features: bfloat16 [8, 1024, 64, 512], P('dp', 'space'), may hold values from -50 to 50
- owners: int32 [8, 1024, 1], P('dp', 'space'), may hold values from 0 to 31; in each aligned block of 32 rows (0 to 31, 32 to 63, ..., all dimensions but the last counted through in order) at most 2 rows name the same one
- neighbors: int32 [8, 1024, 3], P('dp', 'space'), may hold values from -1 to 1022, as said below
- w_reduce: bfloat16 [512, 128], replicated, may hold values from -0.25 to 0.25
- w_spatial: bfloat16 [1152, 128], replicated, may hold values from -0.1875 to 0.1875
- w_expand: bfloat16 [128, 512], replicated, may hold values from -0.5 to 0.5
- w_short: bfloat16 [512, 512], replicated, may hold values from -0.25 to 0.25
- gains_mid: float32 [2, 128], replicated, may hold values from 0.25 to 1.75
- shifts_mid: float32 [2, 128], replicated, may hold values from -2.5 to 2.5
- gains_wide: float32 [2, 512], replicated, may hold values from 0.25 to 1.75
- shifts_wide: float32 [2, 512], replicated, may hold values from -2.5 to 2.5
- cotangent: bfloat16 [8, 2048, 16, 512], P('dp', 'space'), may hold values from -6 to 6
Outputs:
- block_out: bfloat16 [8, 2048, 16, 512], P('dp', 'space')
- grad_features: bfloat16 [8, 1024, 64, 512], P('dp', 'space')
- grad_reduce: float32 [512, 128], P('space')
- grad_spatial: float32 [1152, 128], P('space')
- grad_expand: float32 [128, 512], P('space')
- grad_short: float32 [512, 512], P('space')
- grad_gains_mid: float32 [2, 128], P(None, 'space')
- grad_shifts_mid: float32 [2, 128], P(None, 'space')
- grad_gains_wide: float32 [2, 512], P(None, 'space')
- grad_shifts_wide: float32 [2, 512], P(None, 'space')
Inputs may be any that keep to these rules, and one draw needn't show every extreme that they name: `owners`: among the 32 tiles of one block no owner is named more than 2 times. `neighbors`: entries are tile indices of the same slide or -1 for none; for tile t every index lies between t - 32 and t - 1.
All inputs are finite; a program needn't handle non-finite values.
Results may differ from a plain program's by a relative error of at most 0.02.
Values may be sent and summed in bfloat16 or wider, within the bound.
No kernel may reach another device: no remote copies, remote signals or barrier semaphores. Data moves between devices by JAX's collectives and lax.ppermute only.
A program may use at most 64 MiB of HBM per device.

v0:
```python
import math

import jax
import jax.numpy as jnp
from jax import lax
from jax.sharding import PartitionSpec as P

GROUPS = 32
SIDE = 8


EPS = 1e-05


def passed_along(shard, axis, by):
    peers = lax.axis_size(axis)
    pairs = [(i, i + by) for i in range(peers) if 0 <= i + by < peers]
    return lax.ppermute(shard, axis, pairs)


def smooth(values):
    return values * jax.nn.sigmoid(values)


def smooth_slope(values):
    sig = jax.nn.sigmoid(values)
    return sig * (1.0 + values * (1.0 - sig))


def group_total(per_channel):
    width = per_channel.shape[-1]
    grouped = per_channel.reshape(per_channel.shape[:-1] + (GROUPS, width // GROUPS))
    return jnp.repeat(jnp.sum(grouped, axis=-1), width // GROUPS, axis=-1)


def moments(conv_out):
    values = conv_out.astype(jnp.float32)
    return jnp.stack([jnp.sum(values, axis=0), jnp.sum(values * values, axis=0)])


def grad_moments(upstream, normed):
    return jnp.stack([jnp.sum(upstream, axis=0), jnp.sum(upstream * normed, axis=0)])


def norm_forward(conv_out, totals, members, gain_row, shift_row):
    center = group_total(totals[0]) / members
    spread = group_total(totals[1]) / members - center * center
    inv_spread = lax.rsqrt(spread + EPS)
    normed = (conv_out.astype(jnp.float32) - center) * inv_spread
    return (normed, normed * gain_row + shift_row, center, inv_spread)


def norm_backward(upstream, normed, inv_spread, gain_row, totals, members):
    first = group_total(gain_row * totals[0]) / members
    second = group_total(gain_row * totals[1]) / members
    return inv_spread * (gain_row * upstream - first - normed * second)


def slide_total(partial_sums):
    return lax.psum(partial_sums, "space")


def body(
    features,
    owners,
    neighbors,
    w_reduce,
    w_spatial,
    w_expand,
    w_short,
    gains_mid,
    shifts_mid,
    gains_wide,
    shifts_wide,
    cotangent,
):
    spaces = lax.axis_size("space")
    my_index = lax.axis_index("space")
    tile_count = features.shape[1]
    positions = SIDE * SIDE
    half = SIDE // 2
    quarter = half * half
    width_in = features.shape[3]
    width_mid = w_reduce.shape[1]
    tiles_total = tile_count * spaces
    slide_count = features.shape[0] * lax.axis_size("dp")
    capacity = cotangent.shape[1] // spaces
    members_in = tiles_total * positions * (width_mid // GROUPS)
    members_mid = tiles_total * quarter * (width_mid // GROUPS)
    members_wide = tiles_total * quarter * (width_in // GROUPS)
    row_width = SIDE * width_mid
    cot_owned = cotangent[0].reshape(spaces, capacity, quarter * width_in)
    cot_home = lax.all_to_all(cot_owned, "space", split_axis=0, concat_axis=0, tiled=True)
    flat_in = features[0].reshape(tile_count * positions, width_in)
    conv_one = jnp.dot(flat_in, w_reduce, preferred_element_type=jnp.float32).astype(jnp.bfloat16)
    totals_one = slide_total(moments(conv_one))
    normed_one, pre_one, center_one, scale_one = norm_forward(
        conv_one, totals_one, members_in, gains_mid[0], shifts_mid[0]
    )
    act_one = smooth(pre_one).astype(jnp.bfloat16)
    grid_source = act_one.reshape(tile_count, SIDE, SIDE, width_mid)
    own_rims = jnp.concatenate(
        [grid_source[:, SIDE - 1], grid_source[:, :, SIDE - 1]], axis=1
    ).reshape(tile_count, 2 * row_width)
    prior_rims = passed_along(own_rims, "space", 1)
    rim_pool = jnp.concatenate([prior_rims, own_rims], axis=0)
    links = neighbors[0]
    first_index = (my_index - 1) * tile_count
    pool_slots = jnp.arange(2 * tile_count, dtype=jnp.int32)

    def pick_matrix(column):
        target = links[:, column]
        return (target[:, None] - first_index == pool_slots[None, :]) & (target[:, None] >= 0)

    match_top = pick_matrix(0)
    match_left = pick_matrix(1)
    match_corner = pick_matrix(2)
    top_row = (
        jnp.dot(
            match_top.astype(jnp.bfloat16),
            rim_pool[:, :row_width],
            preferred_element_type=jnp.float32,
        )
        .astype(jnp.bfloat16)
        .reshape(tile_count, SIDE, width_mid)
    )
    left_col = (
        jnp.dot(
            match_left.astype(jnp.bfloat16),
            rim_pool[:, row_width:],
            preferred_element_type=jnp.float32,
        )
        .astype(jnp.bfloat16)
        .reshape(tile_count, SIDE, width_mid)
    )
    corner_cell = jnp.dot(
        match_corner.astype(jnp.bfloat16),
        rim_pool[:, row_width - width_mid : row_width],
        preferred_element_type=jnp.float32,
    ).astype(jnp.bfloat16)
    grid_act = act_one.reshape(tile_count, SIDE, SIDE, width_mid)
    first_line = jnp.concatenate([corner_cell[:, None], top_row], axis=1)
    lower_rows = jnp.concatenate([left_col[:, :, None], grid_act], axis=2)
    padded = jnp.concatenate([first_line[:, None], lower_rows], axis=1)
    columns = jnp.concatenate(
        [
            padded[
                :, offset_row : offset_row + SIDE - 1 : 2, offset_col : offset_col + SIDE - 1 : 2
            ]
            for offset_row in range(3)
            for offset_col in range(3)
        ],
        axis=-1,
    ).reshape(tile_count * quarter, 9 * width_mid)
    conv_two = jnp.dot(columns, w_spatial, preferred_element_type=jnp.float32).astype(jnp.bfloat16)
    totals_two = slide_total(moments(conv_two))
    normed_two, pre_two, center_two, scale_two = norm_forward(
        conv_two, totals_two, members_mid, gains_mid[1], shifts_mid[1]
    )
    act_two = smooth(pre_two).astype(jnp.bfloat16)
    conv_three = jnp.dot(act_two, w_expand, preferred_element_type=jnp.float32).astype(jnp.bfloat16)
    sub_in = (
        features[0]
        .reshape(tile_count, SIDE, SIDE, width_in)[:, ::2, ::2]
        .reshape(tile_count * quarter, width_in)
    )
    conv_short = jnp.dot(sub_in, w_short, preferred_element_type=jnp.float32).astype(jnp.bfloat16)
    totals_wide = slide_total(jnp.concatenate([moments(conv_three), moments(conv_short)], axis=0))
    normed_three, pre_three, center_three, scale_three = norm_forward(
        conv_three, totals_wide[:2], members_wide, gains_wide[0], shifts_wide[0]
    )
    normed_short, pre_short, center_short, scale_short = norm_forward(
        conv_short, totals_wide[2:], members_wide, gains_wide[1], shifts_wide[1]
    )
    summed = pre_three + pre_short
    result = smooth(summed).astype(jnp.bfloat16)
    owner_of = owners[0][:, 0]
    owner_hits = (owner_of[:, None] == jnp.arange(spaces, dtype=jnp.int32)[None, :]).astype(
        jnp.int32
    )
    before = jnp.cumsum(owner_hits, axis=0) - owner_hits
    rank_in = jnp.sum(before * owner_hits, axis=1)
    slot_of = owner_of * capacity + rank_in
    dispatch = (jnp.arange(spaces * capacity, dtype=jnp.int32)[:, None] == slot_of[None, :]).astype(
        jnp.bfloat16
    )
    outgoing = (
        jnp.dot(
            dispatch,
            result.reshape(tile_count, quarter * width_in),
            preferred_element_type=jnp.float32,
        )
        .astype(jnp.bfloat16)
        .reshape(spaces, capacity, quarter * width_in)
    )
    arrived = lax.all_to_all(outgoing, "space", split_axis=0, concat_axis=0, tiled=True)
    block_out = arrived.reshape(1, spaces * capacity, quarter, width_in)
    picked = jnp.dot(
        dispatch.T,
        cot_home.reshape(spaces * capacity, quarter * width_in),
        preferred_element_type=jnp.float32,
    ).reshape(tile_count * quarter, width_in)
    upstream = picked * smooth_slope(summed)
    totals_back = slide_total(
        jnp.concatenate(
            [grad_moments(upstream, normed_three), grad_moments(upstream, normed_short)], axis=0
        )
    )
    dconv_three = norm_backward(
        upstream, normed_three, scale_three, gains_wide[0], totals_back[:2], members_wide
    ).astype(jnp.bfloat16)
    dconv_short = norm_backward(
        upstream, normed_short, scale_short, gains_wide[1], totals_back[2:], members_wide
    ).astype(jnp.bfloat16)
    grad_expand_part = jnp.dot(act_two.T, dconv_three, preferred_element_type=jnp.float32)
    grad_short_part = jnp.dot(sub_in.T, dconv_short, preferred_element_type=jnp.float32)
    back_two = jnp.dot(dconv_three, w_expand.T, preferred_element_type=jnp.float32)
    back_two = back_two * smooth_slope(pre_two)
    totals_two_back = slide_total(grad_moments(back_two, normed_two))
    dconv_two = norm_backward(
        back_two, normed_two, scale_two, gains_mid[1], totals_two_back, members_mid
    ).astype(jnp.bfloat16)
    grad_spatial_part = jnp.dot(columns.T, dconv_two, preferred_element_type=jnp.float32)
    back_cols = jnp.dot(dconv_two, w_spatial.T, preferred_element_type=jnp.float32).reshape(
        tile_count, half, half, 9, width_mid
    )
    back_pad = jnp.zeros((tile_count, SIDE + 1, SIDE + 1, width_mid), jnp.float32)
    for offset_row in range(3):
        for offset_col in range(3):
            back_pad = back_pad.at[
                :, offset_row : offset_row + SIDE - 1 : 2, offset_col : offset_col + SIDE - 1 : 2
            ].add(back_cols[:, :, :, 3 * offset_row + offset_col])
    to_top = back_pad[:, 0, 1:].reshape(tile_count, row_width)
    to_left = back_pad[:, 1:, 0].reshape(tile_count, row_width)
    to_corner = back_pad[:, 0, 0]
    rows_back = jnp.dot(match_top.astype(jnp.float32).T, to_top, precision=lax.Precision.HIGHEST)
    corner_back = jnp.dot(
        match_corner.astype(jnp.float32).T, to_corner, precision=lax.Precision.HIGHEST
    )
    rows_back = rows_back.at[:, row_width - width_mid :].add(corner_back)
    cols_back = jnp.dot(match_left.astype(jnp.float32).T, to_left, precision=lax.Precision.HIGHEST)
    rim_back = jnp.concatenate([rows_back, cols_back], axis=1)
    from_next = passed_along(rim_back[:tile_count].astype(jnp.bfloat16), "space", -1).astype(
        jnp.float32
    )
    own_back = (rim_back[tile_count:] + from_next).reshape(tile_count, 2 * SIDE, width_mid)
    inner = back_pad[:, 1:, 1:]
    inner = inner.at[:, SIDE - 1].add(own_back[:, :SIDE]).at[:, :, SIDE - 1].add(own_back[:, SIDE:])
    back_one = (inner * smooth_slope(pre_one).reshape(tile_count, SIDE, SIDE, width_mid)).reshape(
        tile_count * positions, width_mid
    )
    totals_one_back = slide_total(grad_moments(back_one, normed_one))
    dconv_one = norm_backward(
        back_one, normed_one, scale_one, gains_mid[0], totals_one_back, members_in
    ).astype(jnp.bfloat16)
    grad_reduce_part = jnp.dot(flat_in.T, dconv_one, preferred_element_type=jnp.float32)
    back_in = jnp.dot(dconv_one, w_reduce.T, preferred_element_type=jnp.float32).reshape(
        tile_count, SIDE, SIDE, width_in
    )
    back_short = jnp.dot(dconv_short, w_short.T, preferred_element_type=jnp.float32).reshape(
        tile_count, half, half, width_in
    )
    back_in = back_in.at[:, ::2, ::2].add(back_short)
    grad_features = back_in.reshape(1, tile_count, positions, width_in).astype(jnp.bfloat16)
    gain_mid_full = jnp.stack([totals_one_back[1], totals_two_back[1]])
    shift_mid_full = jnp.stack([totals_one_back[0], totals_two_back[0]])
    gain_wide_full = jnp.stack([totals_back[1], totals_back[3]])
    shift_wide_full = jnp.stack([totals_back[0], totals_back[2]])

    def own_part(array):
        share = array.shape[1] // spaces
        return lax.dynamic_slice_in_dim(array, my_index * share, share, 1)

    whole = (
        lax.psum(grad_reduce_part.astype(jnp.bfloat16), "dp").astype(jnp.float32),
        lax.psum(grad_spatial_part.astype(jnp.bfloat16), "dp").astype(jnp.float32),
        lax.psum(grad_expand_part.astype(jnp.bfloat16), "dp").astype(jnp.float32),
        lax.psum(grad_short_part.astype(jnp.bfloat16), "dp").astype(jnp.float32),
        lax.psum(gain_mid_full.astype(jnp.bfloat16), "dp").astype(jnp.float32),
        lax.psum(shift_mid_full.astype(jnp.bfloat16), "dp").astype(jnp.float32),
        lax.psum(gain_wide_full.astype(jnp.bfloat16), "dp").astype(jnp.float32),
        lax.psum(shift_wide_full.astype(jnp.bfloat16), "dp").astype(jnp.float32),
    )
    shares = (
        lax.psum_scatter(
            whole[0].astype(jnp.bfloat16), "space", scatter_dimension=0, tiled=True
        ).astype(jnp.float32),
        lax.psum_scatter(
            whole[1].astype(jnp.bfloat16), "space", scatter_dimension=0, tiled=True
        ).astype(jnp.float32),
        lax.psum_scatter(
            whole[2].astype(jnp.bfloat16), "space", scatter_dimension=0, tiled=True
        ).astype(jnp.float32),
        lax.psum_scatter(
            whole[3].astype(jnp.bfloat16), "space", scatter_dimension=0, tiled=True
        ).astype(jnp.float32),
    )
    summed_all = (
        shares[0],
        shares[1],
        shares[2],
        shares[3],
        own_part(whole[4]),
        own_part(whole[5]),
        own_part(whole[6]),
        own_part(whole[7]),
    )
    scale_in = 1.0 / math.sqrt(slide_count * tiles_total * positions)
    scale_out = 1.0 / math.sqrt(slide_count * tiles_total * quarter)
    mid_scale = jnp.array([[scale_in], [scale_out]], jnp.float32)
    return (
        block_out,
        grad_features,
        summed_all[0] * scale_in,
        summed_all[1] * scale_out,
        summed_all[2] * scale_out,
        summed_all[3] * scale_out,
        summed_all[4] * mid_scale,
        summed_all[5] * mid_scale,
        summed_all[6] * scale_out,
        summed_all[7] * scale_out,
    )


def solution(mesh):
    placed = (
        P("dp", "space", None, None),
        P("dp", "space", None),
        P("dp", "space", None),
        P(),
        P(),
        P(),
        P(),
        P(),
        P(),
        P(),
        P(),
        P("dp", "space", None, None),
    )
    return jax.shard_map(
        body,
        mesh=mesh,
        in_specs=placed,
        out_specs=(
            P("dp", "space", None, None),
            P("dp", "space", None, None),
            P("space", None),
            P("space", None),
            P("space", None),
            P("space", None),
            P(None, "space"),
            P(None, "space"),
            P(None, "space"),
            P(None, "space"),
        ),
        check_vma=False,
    )
```

profile of v0, /device:TPU:4, one launch (start us, length us, event | category | flops | bytes accessed | tf_op | source)
XLA Modules:
  0.0 1519.2 jit_solution(11342063091150273757)
XLA Ops:
  7.2 2.7 reshape_squeeze.49
  9.9 11.8 all-to-all-start.1
  21.8 2.3 fusion.86
  24.1 81.0 %psum.98 = f32[2,128]{1,0:T(2,128)S(1)} all-reduce(f32[2,128]{1,0:T(2,128)S(1)} %pad_maximum_fusion.7), channel_id=1, replica_groups=mesh['dp'=8,'space'=32] {'space'}, use_global_device_ids=true, to_apply=%region_4.0 | all-reduce | flops 256 | bytes 2048 | tf_op jit(solution)/shard_map/psum | solution.py:60
  109.0 2.9 collective-permute-start
  112.0 37.4 %slice.296 = bf16[32,4,4,128]{3,2,1,0:T(4,128)(2,1)} slice(bf16[32,8,8,128]{3,2,1,0:T(8,128)(2,1)S(1)} %bitcast.217), slice={[0:32:1], [1:8:2], [1:8:2], [0:128:1]} | slice | bytes 262144 | tf_op jit(solution)/shard_map/slice | solution.py:147
  149.4 37.3 %slice.295 = bf16[32,4,4,128]{3,2,1,0:T(4,128)(2,1)} slice(bf16[32,8,8,128]{3,2,1,0:T(8,128)(2,1)S(1)} %bitcast.218), slice={[0:32:1], [1:8:2], [0:7:2], [0:128:1]} | slice | bytes 262144 | tf_op jit(solution)/shard_map/slice | solution.py:147
  186.7 37.3 %slice.293 = bf16[32,4,4,128]{3,2,1,0:T(4,128)(2,1)} slice(bf16[32,8,8,128]{3,2,1,0:T(8,128)(2,1)S(1)} %bitcast.219), slice={[0:32:1], [0:7:2], [1:8:2], [0:128:1]} | slice | bytes 262144 | tf_op jit(solution)/shard_map/slice | solution.py:147
  224.0 37.3 %slice.292 = bf16[32,4,4,128]{3,2,1,0:T(4,128)(2,1)} slice(bf16[32,8,8,128]{3,2,1,0:T(8,128)(2,1)S(1)} %bitcast.220), slice={[0:32:1], [0:7:2], [0:7:2], [0:128:1]} | slice | bytes 262144 | tf_op jit(solution)/shard_map/slice | solution.py:147
  270.9 47.3 %slice.301 = bf16[32,4,4,512]{3,2,1,0:T(4,128)(2,1)S(1)} slice(bf16[32,8,8,512]{3,2,1,0:T(8,128)(2,1)} %bitcast.213), slice={[0:32:1], [0:8:2], [0:8:2], [0:512:1]} | slice | bytes 1048576 | tf_op jit(solution)/shard_map/slice | solution.py:163
  321.1 1.8 convert_reduce_fusion
  324.9 37.4 %slice.290 = bf16[32,4,4,128]{3,2,1,0:T(4,128)(2,1)} slice(bf16[32,9,9,128]{3,2,1,0:T(8,128)(2,1)S(1)} %maximum_maximum_fusion), slice={[0:32:1], [0:7:2], [2:9:2], [0:128:1]} | slice | bytes 262144 | tf_op jit(solution)/shard_map/slice | solution.py:147
  362.2 37.2 %slice.289 = bf16[32,4,4,128]{3,2,1,0:T(4,128)(2,1)} slice(bf16[32,9,9,128]{3,2,1,0:T(8,128)(2,1)S(1)} %maximum_maximum_fusion), slice={[0:32:1], [0:7:2], [1:8:2], [0:128:1]} | slice | bytes 262144 | tf_op jit(solution)/shard_map/slice | solution.py:147
  399.5 37.3 %slice.288 = bf16[32,4,4,128]{3,2,1,0:T(4,128)(2,1)} slice(bf16[32,9,9,128]{3,2,1,0:T(8,128)(2,1)S(1)} %maximum_maximum_fusion), slice={[0:32:1], [0:7:2], [0:7:2], [0:128:1]} | slice | bytes 262144 | tf_op jit(solution)/shard_map/slice | solution.py:147
  437.2 2.9 slice.291
  440.1 4.7 slice.294
  453.8 2.4 reshape.378
  456.8 69.6 %psum.99 = f32[2,128]{1,0:T(2,128)S(1)} all-reduce(f32[2,128]{1,0:T(2,128)S(1)} %pad_maximum_fusion.8), channel_id=1, replica_groups=mesh['dp'=8,'space'=32] {'space'}, use_global_device_ids=true, to_apply=%region_9.0 | all-reduce | flops 256 | bytes 2048 | tf_op jit(solution)/shard_map/psum | solution.py:60
  527.3 2.0 convert_reduce_fusion.1
  529.3 72.8 %psum.100 = f32[4,512]{1,0:T(4,128)S(1)} all-reduce(f32[4,512]{1,0:T(4,128)S(1)} %pad_maximum_fusion.3), channel_id=1, replica_groups=mesh['dp'=8,'space'=32] {'space'}, use_global_device_ids=true, to_apply=%region_16.0 | all-reduce | flops 2048 | bytes 16384 | tf_op jit(solution)/shard_map/psum | solution.py:60
  603.7 2.2 reshape.383
  605.9 2.6 fusion.48
  608.5 2.4 reshape.384
  610.9 3.5 fusion.15
  614.4 70.6 %psum.101 = f32[4,512]{1,0:T(4,128)S(1)} all-reduce(f32[4,512]{1,0:T(4,128)S(1)} %pad_maximum_fusion.4), channel_id=1, replica_groups=mesh['dp'=8,'space'=32] {'space'}, use_global_device_ids=true, to_apply=%region_24.25 | all-reduce | flops 2048 | bytes 16384 | tf_op jit(solution)/shard_map/psum | solution.py:60
  686.6 2.9 fusion.28
  691.3 2.2 fusion.87
  693.5 71.7 %psum.102 = f32[2,128]{1,0:T(2,128)S(1)} all-reduce(f32[2,128]{1,0:T(2,128)S(1)} %pad_maximum_fusion.9), channel_id=1, replica_groups=mesh['dp'=8,'space'=32] {'space'}, use_global_device_ids=true, to_apply=%region_29.30 | all-reduce | flops 256 | bytes 2048 | tf_op jit(solution)/shard_map/psum | solution.py:60
  768.9 73.4 %fusion = bf16[48,128]{1,0:T(8,128)(2,1)} fusion(bf16[1152,128]{1,0:T(8,128)(2,1)} %convolution_convert_fusion.1), kind=kCustom, calls=%all-reduce-scatter | all-reduce-scatter fusion | flops 196609 | bytes 308224
  843.6 6.6 collective-permute-start.8
  850.2 15.4 %collective-permute-start.7 = (bf16[48,128]{1,0:T(8,128)(2,1)}, bf16[48,128]{1,0:T(8,128)(2,1)}, u32[]{:S(2)}, u32[]{:S(2)}) collective-permute-start(bf16[48,128]{1,0:T(8,128)(2,1)} %fusion), channel_id=1, source_target_pairs={{0,6},{1,7},{2,8},{3,9},{4,10},{5,11},{6,12},{7,13},{8,14},{9,15},... | collective-permute-start | bytes 36872
  865.6 1.9 collective-permute-start.6
  867.5 6.3 collective-permute-start.5
  873.8 2.5 fusion.2
  877.7 1.9 fusion.98
  879.6 4.2 reshape.385
  883.8 9.9 fusion.90
  899.6 2.2 scatter_fusion
  901.8 2.2 scatter_fusion.1
  904.0 2.2 scatter_fusion.2
  906.2 2.2 scatter_fusion.3
  908.3 2.2 scatter_fusion.4
  910.5 2.2 scatter_fusion.5
  912.7 2.2 scatter_fusion.6
  920.5 2.0 convolution_convert_fusion
  922.5 2.5 reshape.381
  925.1 6.4 all-to-all-start
  933.1 2.6 collective-permute-start.1
  935.8 4.7 collective-permute-done.1
  940.5 4.4 collective-permute-start.9
  946.8 71.0 %psum.103 = f32[2,128]{1,0:T(2,128)S(1)} all-reduce(f32[2,128]{1,0:T(2,128)S(1)} %pad_maximum_fusion.10), channel_id=1, replica_groups=mesh['dp'=8,'space'=32] {'space'}, use_global_device_ids=true, to_apply=%region_43.44 | all-reduce | flops 256 | bytes 2048 | tf_op jit(solution)/shard_map/psum | solution.py:60
  1019.0 2.1 fusion.4
  1024.3 3.9 collective-permute-start.3
  1028.3 5.7 collective-permute-start.2
  1035.6 4.5 concatenate.99
  1040.8 4.3 copy.88
  1045.1 3.5 scatter_fusion.9
  1048.6 2.5 convert_element_type.164
  1051.2 2.5 copy.89
  1053.7 8.1 all-reduce.6.cloned.1.call-done
  1062.5 197.1 %reduce-scatter.9.cloned.1.call-done = bf16[16,128]{1,0:T(8,128)(2,1)} async-done(((bf16[512,128]{1,0:T(8,128)(2,1)}), bf16[16,128]{1,0:T(8,128)(2,1)}) %reduce-scatter.9.cloned.1.call-update) | async-done | bytes 4112
  1260.4 218.2 %reduce-scatter.11.cloned.1.call-done = bf16[16,512]{1,0:T(8,128)(2,1)} async-done(((bf16[512,512]{1,0:T(8,128)(2,1)}), bf16[16,512]{1,0:T(8,128)(2,1)}) %reduce-scatter.11.cloned.1.call-update) | async-done | bytes 16400
  1479.5 25.6 %all-reduce.3 = (bf16[16,128]{0,1:T(8,128)(2,1)S(1)}, bf16[36,128]{1,0:T(8,128)(2,1)S(1)}, bf16[4,512]{1,0:T(4,128)(2,1)S(1)}, bf16[16,512]{0,1:T(8,128)(2,1)S(1...) all-reduce(bf16[16,128]{0,1:T(8,128)(2,1)S(1)} %copy.93, ...), channel_id=1, replica_groups=mesh['dp'=8,'space'=32] {'dp'}, use_global_device_ids=true, to_apply=%region_49.50 | all-reduce | flops 19456 | bytes 77824 | tf_op jit(solution)/shard_map/psum | solution.py:275
  1509.7 2.6 reshape.382
  (370 shorter events, 67.1 us)
Async XLA Ops:
  7.2 313.9 %copy-start = (bf16[512,512]{1,0:T(8,128)(2,1)S(1)}, bf16[512,512]{1,0:T(8,128)(2,1)}, u32[]{:S(2)}) copy-start(bf16[512,512]{1,0:T(8,128)(2,1)} %param.25) | copy-start | bytes 1572868
  9.9 11.8 copy-start.10
  9.9 593.8 %all-to-all-start.1 = ((bf16[32,2,8192]{2,1,0:T(2,128)(2,1)}), bf16[32,2,8192]{2,1,0:T(2,128)(2,1)}, u32[]{:S(2)}, u32[]{:S(2)}) async-start(bf16[32,2,8192]{2,1,0:T(2,128)(2,1)} %reshape_squeeze.49), calls=%async_computation.1 | async-start | bytes 2097152 | tf_op jit(solution)/shard_map/all_to_all | solution.py:93
  21.7 1040.1 %all-reduce.6.cloned.1.call-start = ((), (), s32[]{:S(2)}) async-start(), calls=%async_computation.6 | async-start | bytes 262144
  21.7 84.2 %copy-start.47 = (f32[2,128]{1,0:T(2,128)S(1)}, f32[2,128]{1,0:T(2,128)}, u32[]{:S(2)}) copy-start(f32[2,128]{1,0:T(2,128)} %param.26) | copy-start | bytes 3076
  21.7 84.2 %copy-start.58 = (f32[2,128]{1,0:T(2,128)S(1)}, f32[2,128]{1,0:T(2,128)}, u32[]{:S(2)}) copy-start(f32[2,128]{1,0:T(2,128)} %param.27) | copy-start | bytes 3076
  108.0 154.0 %copy-start.57 = (s32[1,32,3]{1,0,2:T(1,128)S(1)}, s32[1,32,3]{1,0,2:T(1,128)}, u32[]{:S(2)}) copy-start(s32[1,32,3]{1,0,2:T(1,128)} %param.21) | copy-start | bytes 1156
  108.0 155.1 %copy-start.46 = (f32[2,512]{1,0:T(2,128)S(1)}, f32[2,512]{1,0:T(2,128)}, u32[]{:S(2)}) copy-start(f32[2,512]{1,0:T(2,128)} %param.29) | copy-start | bytes 12292
  108.0 155.7 %copy-start.25 = (f32[2,512]{1,0:T(2,128)S(1)}, f32[2,512]{1,0:T(2,128)}, u32[]{:S(2)}) copy-start(f32[2,512]{1,0:T(2,128)} %param.28) | copy-start | bytes 12292
  108.0 162.1 %copy-start.51 = (s32[1,32,1]{1,2,0:T(1,128)S(1)}, s32[1,32,1]{1,2,0:T(1,128)}, u32[]{:S(2)}) copy-start(s32[1,32,1]{1,2,0:T(1,128)} %param.20) | copy-start | bytes 388
  109.0 214.6 %collective-permute-start = (bf16[32,2048]{1,0:T(8,128)(2,1)}, bf16[32,2048]{1,0:T(8,128)(2,1)S(1)}, u32[]{:S(2)}, u32[]{:S(2)}) collective-permute-start(bf16[32,2048]{1,0:T(8,128)(2,1)} %bitcast.208), channel_id=1, source_target_pairs={{0,1},{1,2},{2,3},{3,4},{4,5},{5,6},{6,7},{7,8},{8,9},{9,10},{10,1... | collective-permute-start | bytes 393224 | tf_op jit(solution)/shard_map/ppermute | solution.py:18
  318.3 5.2 copy-start.11
  318.3 4.6 copy-start.52
  318.4 4.6 copy-start.62
  437.1 13.2 copy-start.16
  437.2 13.9 copy-start.15
  437.2 15.3 %copy-start.14 = (bf16[32,4,4,128]{3,2,1,0:T(4,128)(2,1)S(1)}, bf16[32,4,4,128]{3,2,1,0:T(4,128)(2,1)}, u32[]{:S(2)}) copy-start(bf16[32,4,4,128]{3,2,1,0:T(4,128)(2,1)} %slice.295) | copy-start | bytes 393220
  437.2 16.0 %copy-start.13 = (bf16[32,4,4,128]{3,2,1,0:T(4,128)(2,1)S(1)}, bf16[32,4,4,128]{3,2,1,0:T(4,128)(2,1)}, u32[]{:S(2)}) copy-start(bf16[32,4,4,128]{3,2,1,0:T(4,128)(2,1)} %slice.296) | copy-start | bytes 393220
  453.1 3.1 copy-start.6
  456.2 71.0 %copy-start.55 = (f32[128]{0:T(128)S(1)}, f32[128]{0:T(128)}, u32[]{:S(2)}) copy-start(f32[128]{0:T(128)} %get-tuple-element.173) | copy-start | bytes 1540
  456.2 71.0 %copy-start.65 = (f32[128]{0:T(128)S(1)}, f32[128]{0:T(128)}, u32[]{:S(2)}) copy-start(f32[128]{0:T(128)} %get-tuple-element.163) | copy-start | bytes 1540
  456.7 146.0 %copy-start.8 = (f32[512,128]{1,0:T(8,128)}, f32[512,128]{1,0:T(8,128)S(1)}, u32[]{:S(2)}) copy-start(f32[512,128]{1,0:T(8,128)S(1)} %get-tuple-element.168) | copy-start | bytes 786436
  456.8 72.6 %copy-start.53 = (f32[512]{0:T(512)S(1)}, f32[512]{0:T(512)}, u32[]{:S(2)}) copy-start(f32[512]{0:T(512)} %get-tuple-element.83) | copy-start | bytes 6148
  456.8 72.5 %copy-start.54 = (f32[512]{0:T(512)S(1)}, f32[512]{0:T(512)}, u32[]{:S(2)}) copy-start(f32[512]{0:T(512)} %get-tuple-element.84) | copy-start | bytes 6148
  527.3 164.1 %copy-start.67 = (f32[128]{0:T(128)}, f32[128]{0:T(128)S(1)}, u32[]{:S(2)}) copy-start(f32[128]{0:T(128)S(1)} %add_rsqrt_fusion.2) | copy-start | bytes 1540
  529.3 76.6 %copy-start.50 = (s32[32]{0:T(128)S(1)}, s32[32]{0:T(128)}, u32[]{:S(2)}) copy-start(s32[32]{0:T(128)} %multiply_add_fusion.2) | copy-start | bytes 388
  610.9 74.1 %copy-start.26 = (f32[2,512]{1,0:T(2,128)S(1)}, f32[2,512]{1,0:T(2,128)}, u32[]{:S(2)}) copy-start(f32[2,512]{1,0:T(2,128)} %param.28) | copy-start | bytes 12292
  685.1 4.5 copy-start.21
  686.6 3.8 copy-start.9
  686.6 3.8 copy-start.56
  686.6 3.8 copy-start.66
  691.3 73.9 %copy-start.48 = (f32[2,128]{1,0:T(2,128)S(1)}, f32[2,128]{1,0:T(2,128)}, u32[]{:S(2)}) copy-start(f32[2,128]{1,0:T(2,128)} %param.26) | copy-start | bytes 3076
  768.9 107.3 %copy-start.5 = (bf16[512,512]{1,0:T(8,128)(2,1)S(1)}, bf16[512,512]{1,0:T(8,128)(2,1)}, u32[]{:S(2)}) copy-start(bf16[512,512]{1,0:T(8,128)(2,1)} %get-tuple-element.128) | copy-start | bytes 1572868
  843.6 180.7 %collective-permute-start.8 = (bf16[48,128]{1,0:T(8,128)(2,1)}, bf16[48,128]{1,0:T(8,128)(2,1)}, u32[]{:S(2)}, u32[]{:S(2)}) collective-permute-start(bf16[48,128]{1,0:T(8,128)(2,1)} %fusion), channel_id=1, source_target_pairs={{0,7},{1,8},{2,9},{3,10},{4,11},{5,12},{6,13},{7,14},{8,15},{9,16}... | collective-permute-start | bytes 36872
  850.2 178.1 %collective-permute-start.7 = (bf16[48,128]{1,0:T(8,128)(2,1)}, bf16[48,128]{1,0:T(8,128)(2,1)}, u32[]{:S(2)}, u32[]{:S(2)}) collective-permute-start(bf16[48,128]{1,0:T(8,128)(2,1)} %fusion), channel_id=1, source_target_pairs={{0,6},{1,7},{2,8},{3,9},{4,10},{5,11},{6,12},{7,13},{8,14},{9,15},... | collective-permute-start | bytes 36872
  865.6 169.3 %collective-permute-start.6 = (bf16[48,128]{1,0:T(8,128)(2,1)}, bf16[48,128]{1,0:T(8,128)(2,1)}, u32[]{:S(2)}, u32[]{:S(2)}) collective-permute-start(bf16[48,128]{1,0:T(8,128)(2,1)} %fusion), channel_id=1, source_target_pairs={{0,5},{1,6},{2,7},{3,8},{4,9},{5,10},{6,11},{7,12},{8,13},{9,14},{... | collective-permute-start | bytes 36872
  867.5 167.5 %collective-permute-start.5 = (bf16[48,128]{1,0:T(8,128)(2,1)}, bf16[48,128]{1,0:T(8,128)(2,1)}, u32[]{:S(2)}, u32[]{:S(2)}) collective-permute-start(bf16[48,128]{1,0:T(8,128)(2,1)} %fusion), channel_id=1, source_target_pairs={{0,4},{1,5},{2,6},{3,7},{4,8},{5,9},{6,10},{7,11},{8,12},{9,13},{1... | collective-permute-start | bytes 36872
  925.1 6.7 copy-start.18
  925.1 6.8 copy-start.39
  925.1 6.8 copy-start.43
  925.1 7.2 copy-start.17
  925.1 7.3 copy-start.37
  925.1 7.3 copy-start.41
  925.1 7.7 copy-start.61
  925.1 7.7 copy-start.64
  925.1 584.6 %all-to-all-start = ((bf16[32,2,8192]{2,1,0:T(2,128)(2,1)}), bf16[32,2,8192]{2,1,0:T(2,128)(2,1)}, u32[]{:S(2)}, u32[]{:S(2)}) async-start(bf16[32,2,8192]{2,1,0:T(2,128)(2,1)} %reshape.381), calls=%async_computation | async-start | bytes 2097152 | tf_op jit(solution)/shard_map/all_to_all | solution.py:196
  931.5 4.2 copy-start.22
  931.5 9.0 copy-start.27
  931.5 328.1 %reduce-scatter.9.cloned.1.call-start = ((), (), s32[]{:S(2)}) async-start(), calls=%async_computation.4 | async-start | bytes 135168
  933.1 11.9 copy-start.2
  933.1 7.3 collective-permute-start.1
  935.8 9.4 copy-start.3
  940.5 82.5 %collective-permute-start.9 = (bf16[36,128]{1,0:T(8,128)(2,1)S(1)}, bf16[36,128]{1,0:T(8,128)(2,1)S(1)}, u32[]{:S(2)}, u32[]{:S(2)}) collective-permute-start(bf16[36,128]{1,0:T(8,128)(2,1)S(1)} %copy-done.27), channel_id=1, source_target_pairs={{0,8},{1,9},{2,10},{3,11},{4,12},{5,13},{6,14},{7,15},{8,16},{9,17... | collective-permute-start | bytes 27656
  946.5 71.3 %copy-start.49 = (f32[2,128]{1,0:T(2,128)S(1)}, f32[2,128]{1,0:T(2,128)}, u32[]{:S(2)}) copy-start(f32[2,128]{1,0:T(2,128)} %param.26) | copy-start | bytes 3076
  946.5 72.2 %copy-start.45 = (f32[128]{0:T(128)S(1)}, f32[128]{0:T(128)}, u32[]{:S(2)}) copy-start(f32[128]{0:T(128)} %copy-done.44) | copy-start | bytes 1540
  1018.9 3.0 copy-start.12
  1021.1 12.9 copy-start.4
  1021.9 456.8 %reduce-scatter.11.cloned.1.call-start = ((), (), s32[]{:S(2)}) async-start(), calls=%async_computation.5 | async-start | bytes 540672
  1023.0 12.0 collective-permute-start.4
  1024.3 10.7 collective-permute-start.3
  1028.3 7.3 collective-permute-start.2
  1040.8 4.3 copy-start.20
  1051.2 456.7 %copy-start.59 = (f32[2]{0:T(128)S(1)}, f32[2]{0:T(128)}, u32[]{:S(2)}) copy-start(f32[2]{0:T(128)} %constant.157) | copy-start | bytes 28
  1505.8 6.4 copy-start.1
  (19 other events, 38.7 us)
Sparse Core Ops, SparseCore 0:
  920.4 141.3 all-reduce.5
  1065.4 194.1 reduce-scatter.8
  1264.0 214.5 reduce-scatter.10
where the time goes:
time: 1530 us; the launch traced here: 1520 us
  blocking collectives  536 us (35%)
  waiting for transfers between devices  429 us (28%)
  local copies, waits for them, and re-layouts  399 us (26%)
  starting transfers between devices  69.4 us (5%)
  other arithmetic  43.4 us (3%)
  matrix products  25.9 us (2%)
  between operations  17.1 us (1%)
    psum x6, blocking collectives, slide_total(): return lax.psum(partial_sums, 'space')  437 us
    unnamed x14, waiting for transfers between devices  424 us
    slice x9, local copies, waits for them, and re-layouts, body(): padded[:, offset_row:offset_row + SIDE - 1:2, offset_col:offset_col + SID...  269 us
    unnamed x1, blocking collectives  73.4 us
    slice x1, local copies, waits for them, and re-layouts, body(): features[0].reshape(tile_count, SIDE, SIDE, width_in)[:, ::2, ::2]  47.3 us
    unnamed x11, starting transfers between devices  45.8 us
  transfers between devices with their start and end apart: 15, of which 5 were waited for; matrix products, arithmetic and copies ran while one was open for 29% of the time, Pallas kernels for 0%

commit v1 on v0

v1 whole, which is shorter than its diff:
```python
import functools
import math

import jax
import jax.numpy as jnp
from jax import lax
from jax.experimental import pallas as pl
from jax.experimental.pallas import tpu as pltpu
from jax.sharding import PartitionSpec as P

GROUPS = 32
SIDE = 8
HALF = SIDE // 2
QUARTER = HALF * HALF
POSITIONS = SIDE * SIDE
LANES = 128
EPS = 1e-05
F32 = jnp.float32
BF16 = jnp.bfloat16
I32 = jnp.int32
STAT_ROW = 128
HALF_ROWS = 64
SUM_ROWS = HALF_ROWS + 16
RIMS = [(SIDE - 1) * SIDE + c for c in range(SIDE)] + [r * SIDE + SIDE - 1 for r in range(SIDE)]


def struct(shape, dtype):
    return jax.ShapeDtypeStruct(shape, dtype)


def far(shape, dtype):
    return pltpu.HBM(shape, dtype)


def small_grant():
    return pltpu.CompilerParams(vmem_limit_bytes=24 << 20)


def held(array):
    return pltpu.with_memory_space_constraint(array, pltpu.HBM)


def whole(shape):
    return pl.BlockSpec(tuple(shape), lambda g: (0,) * len(shape))


def run(kernel, outs, args, scratch=(), scalars=(), specs=None, near=()):
    specs = specs or {}
    args = [arg if k in near or k in scalars else held(arg) for k, arg in enumerate(args)]
    smem = pl.BlockSpec(memory_space=pltpu.SMEM)
    in_specs = [
        smem if k in scalars else specs.get(k) or whole(arg.shape) for k, arg in enumerate(args)
    ]
    return pl.pallas_call(
        kernel,
        grid=(1,),
        out_shape=outs,
        in_specs=in_specs,
        out_specs=[whole(out.shape) for out in outs],
        scratch_shapes=list(scratch),
        compiler_params=small_grant(),
    )(*args)


def lane_of(shape):
    return lax.broadcasted_iota(I32, shape, len(shape) - 1)


def row_of(shape):
    return lax.broadcasted_iota(I32, shape, len(shape) - 2)


def onehot(mask, dtype=BF16):
    return jnp.where(mask, 1.0, 0.0).astype(dtype)


def exact_dot(a, b, dims):
    return lax.dot_general(
        a, b, (dims, ((), ())), precision=lax.Precision.HIGHEST, preferred_element_type=F32
    )


def dot(a, b, dims=((1,), (0,))):
    return lax.dot_general(a, b, (dims, ((), ())), preferred_element_type=F32)


def group_matrix(width):
    shift = (width // GROUPS).bit_length() - 1
    shape = (width, LANES)
    return onehot((row_of(shape) >> shift) == (lane_of(shape) & (GROUPS - 1)), F32)


def lane_blocks():
    shape = (8, LANES)
    return (lane_of(shape) >> 5) == row_of(shape)


def rows8(rows):
    shape = (8, rows[0].shape[-1])
    place = row_of(shape)
    total = jnp.zeros(shape, F32)
    for k, row in enumerate(rows):
        total = jnp.where(place == k, jnp.broadcast_to(row, shape), total)
    return total


def group_line(rows):
    groups = exact_dot(rows, group_matrix(rows.shape[-1]), ((1,), (0,)))
    return jnp.sum(jnp.where(lane_blocks(), groups, 0.0), axis=0, keepdims=True)


def pack(rows, out_ref):
    line = group_line(rows)
    out_ref[...] = jnp.broadcast_to(line.reshape(1, 1, LANES), out_ref.shape)


def pack_thin(rows, out_ref):
    line = group_line(rows)
    high = line.astype(BF16).astype(F32)
    middle = (line - high).astype(BF16).astype(F32)
    low = line - high - middle
    block = rows8([high, middle, low]).astype(BF16)
    shape = (out_ref.shape[0], 8, LANES)
    out_ref[:, STAT_ROW : STAT_ROW + 8, :] = jnp.broadcast_to(block[None], shape)


def unpack(in_ref, width):
    if len(in_ref.shape) == 3 and in_ref.shape[1] == 8:
        line = column_sum(jnp.sum(in_ref[...].astype(F32), axis=0))
    else:
        line = jnp.sum(in_ref[...], axis=0)
    spread = jnp.where(lane_blocks(), jnp.broadcast_to(line, (8, LANES)), 0.0)
    return exact_dot(spread, group_matrix(width), ((1,), (1,)))


def center_scale(total, square, members):
    center = total / members
    spread = square / members - center * center
    return center, lax.rsqrt(spread + EPS)


def column_sum(values):
    return jnp.sum(values, axis=0, keepdims=True)


def gate(values):
    return 1.0 / (1.0 + jnp.exp(-values))


def smooth(values):
    return values * gate(values)


def smooth_slope(values):
    sig = gate(values)
    return sig * (1.0 + values * (1.0 - sig))


def stack_lanes(values, out_ref, rows):
    high = values.shape[1]
    for j in range(values.shape[2] // LANES):
        out_ref[rows, j * high : (j + 1) * high, :] = values[:, :, j * LANES : (j + 1) * LANES]


def reduce_kernel(f_ref, w_ref, cot_ref, c1_ref, rim_ref, s_ref, flat, acc):
    step = pl.program_id(0)
    peers = cot_ref.shape[0]
    stack_lanes(cot_ref[...], s_ref, pl.ds(step * peers, peers))
    tiles = f_ref.shape[0] // POSITIONS
    conv = dot(f_ref[...], w_ref[...]).astype(BF16).astype(F32)
    flat[...] = conv

    @pl.when(step == 0)
    def _():
        acc[...] = jnp.zeros(acc.shape, F32)

    acc[...] += rows8([column_sum(conv), column_sum(conv * conv)])
    for p in range(POSITIONS):
        c1_ref[p] = flat[pl.ds(p, tiles, stride=POSITIONS), :].astype(BF16)
    for k, p in enumerate(RIMS):
        rim_ref[k] = c1_ref[p]

    @pl.when(step == pl.num_programs(0) - 1)
    def _():
        pack_thin(acc[...], s_ref)


def pick_rows(shape, across):
    out, src = (row_of(shape), lane_of(shape)) if not across else (lane_of(shape), row_of(shape))
    q = out & (QUARTER - 1)
    place = ((out >> 4) << 6) + ((q >> 2) << 4) + ((q & 3) << 1)
    return onehot(place == src)


def short_kernel(f_ref, w_ref, sub_ref, cs_ref, ms_ref):
    step = pl.program_id(0)
    picked = pick_rows((4 * QUARTER, 4 * POSITIONS), False)
    for g in range(f_ref.shape[0] // (4 * POSITIONS)):
        block = f_ref[g * 4 * POSITIONS : (g + 1) * 4 * POSITIONS, :]
        sub_ref[g * 4 * QUARTER : (g + 1) * 4 * QUARTER, :] = dot(picked, block).astype(BF16)
    conv = dot(sub_ref[...], w_ref[...]).astype(BF16)
    cs_ref[...] = conv
    conv = conv.astype(F32)

    @pl.when(step == 0)
    def _():
        ms_ref[...] = jnp.zeros(ms_ref.shape, F32)

    zero = jnp.zeros((1, conv.shape[1]), F32)
    ms_ref[...] += rows8([zero, zero, column_sum(conv), column_sum(conv * conv)])


def spatial_kernel(
    members, c1_ref, prior_ref, g_ref, link_ref, gain_ref, shift_ref, w_ref, c2_ref, col_ref, v_ref, s_ref, act
):
    tiles = c1_ref.shape[1]
    width = c1_ref.shape[2]
    totals = unpack(g_ref, width)
    center, scale = center_scale(totals[0:1], totals[1:2], members)
    v_ref[...] = rows8([center, scale])
    gain, shift = gain_ref[0:1, :], shift_ref[0:1, :]
    factor = scale * gain
    offset = shift - center * factor

    def activated(raw):
        return smooth(raw.astype(F32) * factor + offset).astype(BF16)

    for p in range(POSITIONS):
        act[p] = activated(c1_ref[p])
    pool = [
        jnp.concatenate([activated(prior_ref[k]), act[p]], axis=0) for k, p in enumerate(RIMS)
    ]
    slots = lane_of((tiles, 2 * tiles))

    def chosen(column, parts):
        match = onehot(link_ref[:, column : column + 1] == slots)
        return dot(match, jnp.concatenate(parts, axis=1)).astype(BF16)

    top = chosen(0, pool[:SIDE])
    left = chosen(1, pool[SIDE:])
    corner = chosen(2, pool[SIDE - 1 : SIDE])

    def padded(row, col):
        if row == 0 and col == 0:
            return corner
        if row == 0:
            return top[:, (col - 1) * width : col * width]
        if col == 0:
            return left[:, (row - 1) * width : row * width]
        return act[(row - 1) * SIDE + col - 1]

    for i in range(HALF):
        for j in range(HALF):
            q = i * HALF + j
            for k in range(9):
                col_ref[q * tiles : (q + 1) * tiles, k * width : (k + 1) * width] = padded(
                    2 * i + k // 3, 2 * j + k % 3
                )
    conv = dot(col_ref[...], w_ref[...]).astype(BF16)
    c2_ref[...] = conv
    conv = conv.astype(F32)
    pack(rows8([column_sum(conv), column_sum(conv * conv)]), s_ref)


def expand_kernel(
    members, c2_ref, g_ref, gain_ref, shift_ref, w_ref, ms_ref, act_ref, c3_ref, v_ref, s_ref, flat
):
    width = c2_ref.shape[1]
    tiles = c2_ref.shape[0] // QUARTER
    totals = unpack(g_ref, width)
    center, scale = center_scale(totals[0:1], totals[1:2], members)
    v_ref[...] = rows8([center, scale])
    normed = (c2_ref[...].astype(F32) - center) * scale
    flat[...] = smooth(normed * gain_ref[1:2, :] + shift_ref[1:2, :])
    for t in range(tiles):
        act_ref[t * QUARTER : (t + 1) * QUARTER, :] = flat[pl.ds(t, QUARTER, stride=tiles), :].astype(
            BF16
        )
    conv = dot(act_ref[...], w_ref[...]).astype(BF16)
    c3_ref[...] = conv
    conv = conv.astype(F32)
    pack(rows8([column_sum(conv), column_sum(conv * conv)]) + ms_ref[...], s_ref)


def join_kernel(
    members,
    capacity,
    owner_ref,
    c3_ref,
    cs_ref,
    g_ref,
    gain_ref,
    shift_ref,
    cot_ref,
    out_ref,
    up_ref,
    v_ref,
    sum_ref,
    counts,
    slots,
):
    width = c3_ref.shape[1]
    tiles = owner_ref.shape[0]

    def clear(k, carry):
        counts[k] = 0
        return carry

    lax.fori_loop(0, counts.shape[0], clear, 0)

    def place(t, carry):
        owner = owner_ref[t]
        rank = counts[owner]
        counts[owner] = rank + 1
        slots[t] = rank
        return carry

    lax.fori_loop(0, tiles, place, 0)
    totals = unpack(g_ref, width)
    center_three, scale_three = center_scale(totals[0:1], totals[1:2], members)
    center_short, scale_short = center_scale(totals[2:3], totals[3:4], members)
    v_ref[...] = rows8([center_three, scale_three, center_short, scale_short])
    gain_three, gain_short = gain_ref[0:1, :], gain_ref[1:2, :]
    shift = shift_ref[0:1, :] + shift_ref[1:2, :]
    out_ref[:, 0:STAT_ROW, :] = jnp.zeros((out_ref.shape[0], STAT_ROW, LANES), BF16)
    high = capacity * QUARTER

    def fold(values):
        return values[:8] + values[8:]

    def tile(t, sums):
        rows = pl.ds(pl.multiple_of(t * QUARTER, QUARTER), QUARTER)
        owner = owner_ref[t]
        start = pl.multiple_of(slots[t] * QUARTER, QUARTER)
        three = (c3_ref[rows, :].astype(F32) - center_three) * scale_three
        short = (cs_ref[rows, :].astype(F32) - center_short) * scale_short
        summed = three * gain_three + short * gain_short + shift
        sig = gate(summed)
        result = (summed * sig).astype(BF16)
        picked = []
        for j in range(width // LANES):
            place = pl.ds(j * high + start, QUARTER)
            out_ref[owner, place, :] = result[:, j * LANES : (j + 1) * LANES]
            picked.append(cot_ref[owner, place, :])
        upstream = jnp.concatenate(picked, axis=1).astype(F32) * (sig * (1.0 + summed * (1.0 - sig)))
        up_ref[rows, :] = upstream
        return (
            sums[0] + fold(upstream),
            sums[1] + fold(upstream * three),
            sums[2] + fold(upstream * short),
        )

    zero = jnp.zeros((8, width), F32)
    sums = lax.fori_loop(0, tiles, tile, (zero, zero, zero))
    up, three, short = (column_sum(part) for part in sums)
    sum_ref[...] = rows8([three, short, up])
    pack_thin(
        rows8([gain_three * up, gain_three * three, gain_short * up, gain_short * short]), out_ref
    )


def unstack_kernel(in_ref, out_ref):
    high = in_ref.shape[1] * LANES // out_ref.shape[2]
    shape = (out_ref.shape[0], out_ref.shape[1], LANES)
    for j in range(out_ref.shape[2] // LANES):
        part = in_ref[:, j * high : (j + 1) * high, :]
        out_ref[:, :, j * LANES : (j + 1) * LANES] = part.reshape(shape)


def back_two_kernel(
    members,
    c3_ref,
    cs_ref,
    up_ref,
    vw_ref,
    g_ref,
    gain_ref,
    c2_ref,
    v2_ref,
    gain_mid_ref,
    shift_mid_ref,
    w_ref,
    d3_ref,
    ds_ref,
    b2_ref,
    sum_ref,
    s_ref,
    flat,
):
    width = c3_ref.shape[1]
    tiles = c3_ref.shape[0] // QUARTER
    totals = unpack(g_ref, width) / members
    center_three, scale_three = vw_ref[0:1, :], vw_ref[1:2, :]
    center_short, scale_short = vw_ref[2:3, :], vw_ref[3:4, :]
    gain_three, gain_short = gain_ref[0:1, :], gain_ref[1:2, :]
    chunk = 64

    def block(k, carry):
        rows = pl.ds(pl.multiple_of(k * chunk, chunk), chunk)
        up = up_ref[rows, :]
        three = (c3_ref[rows, :].astype(F32) - center_three) * scale_three
        short = (cs_ref[rows, :].astype(F32) - center_short) * scale_short
        d3_ref[rows, :] = (
            scale_three * (gain_three * up - totals[0:1] - three * totals[1:2])
        ).astype(BF16)
        ds_ref[rows, :] = (
            scale_short * (gain_short * up - totals[2:3] - short * totals[3:4])
        ).astype(BF16)
        return carry

    lax.fori_loop(0, c3_ref.shape[0] // chunk, block, 0)
    flat[...] = dot(d3_ref[...], w_ref[...], ((1,), (1,)))
    center, scale = v2_ref[0:1, :], v2_ref[1:2, :]
    gain, shift = gain_mid_ref[1:2, :], shift_mid_ref[1:2, :]
    first = jnp.zeros((tiles, flat.shape[1]), F32)
    second = first
    for q in range(QUARTER):
        rows = slice(q * tiles, (q + 1) * tiles)
        normed = (c2_ref[rows, :].astype(F32) - center) * scale
        back = flat[pl.ds(q, tiles, stride=QUARTER), :] * smooth_slope(normed * gain + shift)
        b2_ref[rows, :] = back
        first = first + back
        second = second + back * normed
    first, second = column_sum(first), column_sum(second)
    sum_ref[...] = rows8([first, second])
    pack(rows8([gain * first, gain * second]), s_ref)


def wide_grads_kernel(act_ref, d3_ref, sub_ref, ds_ref, w_ref, ge_ref, gs_ref, bs_ref):
    ge_ref[...] = dot(act_ref[...], d3_ref[...], ((0,), (0,))).astype(BF16)
    gs_ref[...] = dot(sub_ref[...], ds_ref[...], ((0,), (0,))).astype(BF16)
    bs_ref[...] = dot(ds_ref[...], w_ref[...], ((1,), (1,))).astype(BF16)


def back_one_kernel(
    members,
    b2_ref,
    c2_ref,
    v2_ref,
    g_ref,
    gain_ref,
    shift_ref,
    w_ref,
    c1_ref,
    prior_ref,
    v1_ref,
    link_ref,
    d2_ref,
    b1_ref,
    rim_ref,
    sum_ref,
    s_ref,
    taps,
    own,
):
    tiles = c1_ref.shape[1]
    width = c1_ref.shape[2]
    totals = unpack(g_ref, width) / members
    center, scale = v2_ref[0:1, :], v2_ref[1:2, :]
    normed = (c2_ref[...].astype(F32) - center) * scale
    d2_ref[...] = (
        scale * (gain_ref[1:2, :] * b2_ref[...] - totals[0:1] - normed * totals[1:2])
    ).astype(BF16)
    for k in range(9):
        taps[k] = dot(d2_ref[...], w_ref[k * width : (k + 1) * width, :], ((1,), (1,))).reshape(
            QUARTER, tiles, width
        )

    def pad_sum(row, col):
        total = None
        for a in range(3):
            for b in range(3):
                if (row - a) % 2 or (col - b) % 2:
                    continue
                i, j = (row - a) // 2, (col - b) // 2
                if 0 <= i < HALF and 0 <= j < HALF:
                    part = taps[3 * a + b, i * HALF + j]
                    total = part if total is None else total + part
        return total

    slots = row_of((2 * tiles, tiles))

    def returned(column, parts):
        match = onehot(link_ref[column : column + 1, :] == slots)
        values = jnp.concatenate(parts, axis=1)
        high = values.astype(BF16)
        low = (values - high.astype(F32)).astype(BF16)
        return dot(match, high) + dot(match, low)

    rows = returned(0, [pad_sum(0, 1 + c) for c in range(SIDE)])
    cols = returned(1, [pad_sum(1 + r, 0) for r in range(SIDE)])
    corner = returned(2, [pad_sum(0, 0)])
    center, scale = v1_ref[0:1, :], v1_ref[1:2, :]
    gain, shift = gain_ref[0:1, :], shift_ref[0:1, :]
    first = jnp.zeros((tiles, width), F32)
    second = first
    for k in range(2 * SIDE):
        source = rows if k < SIDE else cols
        place = k % SIDE
        values = source[:, place * width : (place + 1) * width]
        if k == SIDE - 1:
            values = values + corner
        going = values[:tiles].astype(BF16)
        rim_ref[k] = going
        own[k] = values[tiles:]
        normed = (prior_ref[k].astype(F32) - center) * scale
        away = going.astype(F32) * smooth_slope(normed * gain + shift)
        first = first + away
        second = second + away * normed
    for p in range(POSITIONS):
        row, col = p // SIDE, p % SIDE
        total = pad_sum(row + 1, col + 1)
        if row == SIDE - 1:
            total = total + own[col]
        if col == SIDE - 1:
            total = total + own[SIDE + row]
        normed = (c1_ref[p].astype(F32) - center) * scale
        back = total * smooth_slope(normed * gain + shift)
        b1_ref[p * tiles : (p + 1) * tiles, :] = back
        first = first + back
        second = second + back * normed
    first, second = column_sum(first), column_sum(second)
    sum_ref[...] = rows8([first, second])
    pack(rows8([gain * first, gain * second]), s_ref)


def mid_grads_kernel(
    core_ref, col_ref, d2_ref, ge_ref, gs_ref, wide_ref, two_ref, one_ref, keep_ref, send_ref, flat, blocks, packed
):
    spaces = keep_ref.shape[0]
    width = d2_ref.shape[1]
    share = col_ref.shape[1] // spaces
    flat[0 : col_ref.shape[1], :] = dot(d2_ref[...], col_ref[...], ((0,), (0,))).T
    blocks[...] = jnp.zeros(blocks.shape, F32)

    def spread(row, per, start):
        shape = (spaces, row.shape[1])
        shift = per.bit_length() - 1
        kept = jnp.where((lane_of(shape) >> shift) == row_of(shape), jnp.broadcast_to(row, shape), 0.0)
        shape = (row.shape[1], LANES)
        return dot(
            kept.astype(BF16), onehot((row_of(shape) & (per - 1)) + start == lane_of(shape))
        )

    wide_share = wide_ref.shape[1] // spaces
    mid_share = width // spaces
    line = jnp.zeros((spaces, LANES), F32)
    for k in range(3):
        line = line + spread(wide_ref[k : k + 1, :], wide_share, k * wide_share)
    start = 3 * wide_share
    for k in range(2):
        line = line + spread(one_ref[k : k + 1, :], mid_share, start + 2 * k * mid_share)
        line = line + spread(two_ref[k : k + 1, :], mid_share, start + (2 * k + 1) * mid_share)
    for s in range(spaces):
        blocks[s, 0:share, :] = flat[s * share : (s + 1) * share, :]
        blocks[s, share : share + 1, :] = line[s : s + 1, :]
    shape = (spaces * 16, 4 * ge_ref.shape[0])
    out_row, src = row_of(shape), lane_of(shape)
    wanted = ((out_row >> 4) << 2) + (out_row & 3) + (((out_row & 15) >> 2) << 7)
    parts = jnp.concatenate([ge_ref[:, j * LANES : (j + 1) * LANES] for j in range(4)], axis=0)
    packed[:, 0:16, :] = dot(onehot(wanted == src), parts).astype(BF16).reshape(spaces, 16, LANES)
    for j in range(4):
        packed[:, 16 + 16 * j : 32 + 16 * j, :] = gs_ref[:, j * LANES : (j + 1) * LANES].reshape(
            spaces, 16, LANES
        )
    packed[:, 80:128, :] = blocks[...].astype(BF16)
    mine = pl.multiple_of(core_ref[0] * HALF_ROWS, HALF_ROWS)
    keep_ref[...] = packed[:, pl.ds(mine, HALF_ROWS), :]
    send_ref[...] = packed[:, pl.ds(HALF_ROWS - mine, HALF_ROWS), :]


def first_grad_kernel(
    members, b1_ref, c1_ref, rim_ref, v1_ref, g_ref, gain_ref, shift_ref, f_ref, keep_ref, twin_ref, d1_ref, out_ref, flat
):
    tiles = c1_ref.shape[1]
    width = c1_ref.shape[2]
    spaces = out_ref.shape[0]
    totals = unpack(g_ref, width) / members
    center, scale = v1_ref[0:1, :], v1_ref[1:2, :]
    gain, shift = gain_ref[0:1, :], shift_ref[0:1, :]
    for p in range(POSITIONS):
        row, col = p // SIDE, p % SIDE
        normed = (c1_ref[p].astype(F32) - center) * scale
        back = b1_ref[p * tiles : (p + 1) * tiles, :]
        arriving = None
        if row == SIDE - 1:
            arriving = rim_ref[col].astype(F32)
        if col == SIDE - 1:
            more = rim_ref[SIDE + row].astype(F32)
            arriving = more if arriving is None else arriving + more
        if arriving is not None:
            back = back + arriving * smooth_slope(normed * gain + shift)
        flat[p * tiles : (p + 1) * tiles, :] = scale * (
            gain * back - totals[0:1] - normed * totals[1:2]
        )
    for t in range(tiles):
        d1_ref[t * POSITIONS : (t + 1) * POSITIONS, :] = flat[
            pl.ds(t, POSITIONS, stride=tiles), :
        ].astype(BF16)
    grad = dot(d1_ref[...], f_ref[...], ((0,), (0,))).T
    share = grad.shape[0] // spaces
    out_ref[:, 0:HALF_ROWS, :] = (keep_ref[...].astype(F32) + twin_ref[...].astype(F32)).astype(BF16)
    out_ref[:, HALF_ROWS:SUM_ROWS, :] = grad.astype(BF16).reshape(spaces, share, width)


def features_kernel(d1_ref, w_ref, bs_ref, out_ref):
    back = dot(d1_ref[...], w_ref[...], ((1,), (1,)))
    spread = pick_rows((4 * POSITIONS, 4 * QUARTER), True)
    for g in range(out_ref.shape[0] // (4 * POSITIONS)):
        rows = slice(g * 4 * POSITIONS, (g + 1) * 4 * POSITIONS)
        short = bs_ref[g * 4 * QUARTER : (g + 1) * 4 * QUARTER, :]
        out_ref[rows, :] = (back[rows] + dot(spread, short)).astype(BF16)


def total_kernel(in_ref, out_ref):
    total = in_ref[0].astype(F32)
    for s in range(1, in_ref.shape[0]):
        total = total + in_ref[s].astype(F32)
    total = total.astype(BF16)
    for d in range(out_ref.shape[0]):
        out_ref[d] = total


def final_kernel(
    scale_in, scale_out, in_ref, gr_ref, gp_ref, ge_ref, gs_ref, gm_ref, sm_ref, gw_ref, sw_ref, sums
):
    def added(devices, rows):
        total = None
        for d in devices:
            part = in_ref[d, rows, :].astype(F32)
            total = part if total is None else total + part
        return total

    count = in_ref.shape[0]
    for core in range(2):
        sums[core * HALF_ROWS : (core + 1) * HALF_ROWS, :] = added(
            range(core, count, 2), slice(0, HALF_ROWS)
        )
    sums[128:144, :] = added(range(count), slice(HALF_ROWS, SUM_ROWS))
    gr_ref[...] = sums[128:144, :] * scale_in
    for j in range(4):
        lanes = slice(j * LANES, (j + 1) * LANES)
        ge_ref[:, lanes] = sums[4 * j : 4 * j + 4, :] * scale_out
        gs_ref[:, lanes] = sums[16 + 16 * j : 32 + 16 * j, :] * scale_out
    share = gp_ref.shape[0]
    gp_ref[...] = sums[80 : 80 + share, :] * scale_out
    line = sums[80 + share : 81 + share, :]

    def gathered(start, per):
        shape = (8, LANES)
        shift = per.bit_length() - 1
        moved = lane_of(shape) - start
        kept = jnp.where(
            (moved >= 0) & ((moved >> shift) == row_of(shape)), jnp.broadcast_to(line, shape), 0.0
        )
        shape = (LANES, per)
        return exact_dot(
            kept, onehot(((row_of(shape) - start) & (per - 1)) == lane_of(shape), F32), ((1,), (0,))
        )

    wide_share = gw_ref.shape[1]
    wide = gathered(0, wide_share) * scale_out
    gw_ref[...] = wide[0:2]
    sw_ref[0:1, :] = wide[2:3]
    sw_ref[1:2, :] = wide[2:3]
    mid = gathered(3 * wide_share, gm_ref.shape[1])
    scales = jnp.where((row_of(mid.shape) & 1) == 0, scale_in, scale_out)
    mid = mid * scales
    gm_ref[...] = mid[2:4]
    sm_ref[...] = mid[0:2]


def step(
    features,
    owners,
    neighbors,
    w_reduce,
    w_spatial,
    w_expand,
    w_short,
    gains_mid,
    shifts_mid,
    gains_wide,
    shifts_wide,
    cotangent,
):
    spaces = lax.axis_size("space")
    dps = lax.axis_size("dp")
    my_index = lax.axis_index("space")
    tiles = features.shape[1]
    width_in = features.shape[3]
    width_mid = w_reduce.shape[1]
    tiles_total = tiles * spaces
    slide_count = features.shape[0] * dps
    capacity = cotangent.shape[1] // spaces
    members_in = float(tiles_total * POSITIONS * (width_mid // GROUPS))
    members_mid = float(tiles_total * QUARTER * (width_mid // GROUPS))
    members_wide = float(tiles_total * QUARTER * (width_in // GROUPS))
    fine, coarse = tiles * POSITIONS, tiles * QUARTER
    stat = struct((spaces, 1, LANES), F32)
    carried = struct((spaces, STAT_ROW + 8, LANES), BF16)
    carried_stat = pl.BlockSpec((spaces, 8, LANES), lambda g: (0, STAT_ROW // 8, 0))
    carried_data = pl.BlockSpec((spaces, STAT_ROW, LANES), lambda g: (0, 0, 0))
    vec_mid, vec_wide = struct((8, width_mid), F32), struct((8, width_in), F32)
    sum_mid, sum_wide = far((8, width_mid), F32), far((8, width_in), F32)
    rims = struct((2 * SIDE, tiles, width_mid), BF16)

    def exchanged(array, axis="space"):
        return lax.all_to_all(array, axis, 0, 0, tiled=True)

    links = neighbors[0]
    links = jnp.where(links >= 0, links - (my_index - 1) * tiles, -1).astype(I32)
    links_across = jnp.pad(links.T, ((0, 5), (0, 0)), constant_values=-1)
    owner_of = owners[0].reshape(tiles)
    core = (lax.axis_index("dp") & 1).reshape(1).astype(I32)
    flat_in = features[0].reshape(fine, width_in)

    steps = 2
    grid_rows = fine // steps
    conv_one, own_rims, stat_one = pl.pallas_call(
        reduce_kernel,
        name="reduce",
        compiler_params=small_grant(),
        grid=(steps,),
        in_specs=[
            pl.BlockSpec((grid_rows, width_in), lambda g: (g, 0)),
            pl.BlockSpec((width_in, width_mid), lambda g: (0, 0)),
            pl.BlockSpec((spaces // steps, capacity * QUARTER, width_in), lambda g: (g, 0, 0)),
        ],
        out_specs=[
            pl.BlockSpec((POSITIONS, tiles // steps, width_mid), lambda g: (0, g, 0)),
            pl.BlockSpec((2 * SIDE, tiles // steps, width_mid), lambda g: (0, g, 0)),
            pl.BlockSpec(carried.shape, lambda g: (0, 0, 0)),
        ],
        out_shape=[far((POSITIONS, tiles, width_mid), BF16), rims, carried],
        scratch_shapes=[pltpu.VMEM((grid_rows, width_mid), F32), pltpu.VMEM((8, width_mid), F32)],
    )(held(flat_in), held(w_reduce), held(cotangent[0].reshape(spaces, capacity * QUARTER, width_in)))
    all_one = exchanged(stat_one)
    prior_rims = lax.ppermute(own_rims, "space", [(i, i + 1) for i in range(spaces - 1)])
    sub_in, conv_short, moments_short = pl.pallas_call(
        short_kernel,
        name="short",
        compiler_params=small_grant(),
        grid=(steps,),
        in_specs=[
            pl.BlockSpec((grid_rows, width_in), lambda g: (g, 0)),
            pl.BlockSpec((width_in, width_in), lambda g: (0, 0)),
        ],
        out_specs=[
            pl.BlockSpec((coarse // steps, width_in), lambda g: (g, 0)),
            pl.BlockSpec((coarse // steps, width_in), lambda g: (g, 0)),
            pl.BlockSpec((8, width_in), lambda g: (0, 0)),
        ],
        out_shape=[
            far((coarse, width_in), BF16),
            struct((coarse, width_in), BF16),
            vec_wide,
        ],
    )(held(flat_in), held(w_short))
    conv_two, columns, vec_one, stat_two = run(
        functools.partial(spatial_kernel, members_in),
        [struct((coarse, width_mid), BF16), far((coarse, 9 * width_mid), BF16), vec_mid, stat],
        (conv_one, prior_rims, all_one, links, gains_mid, shifts_mid, w_spatial),
        [pltpu.VMEM((POSITIONS, tiles, width_mid), BF16)],
        specs={2: carried_stat},
        near=(1, 2, 4, 5, 6),
    )
    all_two = exchanged(stat_two)
    act_two, conv_three, vec_two, stat_wide = run(
        functools.partial(expand_kernel, members_mid),
        [far((coarse, width_mid), BF16), struct((coarse, width_in), BF16), vec_mid, stat],
        (conv_two, all_two, gains_mid, shifts_mid, w_expand, moments_short),
        [pltpu.VMEM((coarse, width_mid), F32)],
        near=(0, 1, 2, 3, 4, 5),
    )
    all_wide = exchanged(stat_wide)
    outgoing, upstream, vec_join, sums_wide = run(
        functools.partial(join_kernel, members_wide, capacity),
        [
            carried,
            far((coarse, width_in), F32),
            vec_wide,
            sum_wide,
        ],
        (owner_of, conv_three, conv_short, all_wide, gains_wide, shifts_wide, all_one),
        [pltpu.SMEM((spaces,), I32), pltpu.SMEM((tiles,), I32)],
        (0,),
        {6: carried_data},
        (1, 2, 3, 4, 5),
    )
    all_back = exchanged(outgoing)
    (block_out,) = run(
        unstack_kernel,
        [far((spaces * capacity, QUARTER, width_in), BF16)],
        (all_back,),
        specs={0: carried_data},
        near=(0,),
    )
    dconv_three, dconv_short, back_two, sums_two, stat_two_back = run(
        functools.partial(back_two_kernel, members_wide),
        [
            far((coarse, width_in), BF16),
            far((coarse, width_in), BF16),
            struct((coarse, width_mid), F32),
            sum_mid,
            stat,
        ],
        (
            conv_three,
            conv_short,
            upstream,
            vec_join,
            all_back,
            gains_wide,
            conv_two,
            vec_two,
            gains_mid,
            shifts_mid,
            w_expand,
        ),
        [pltpu.VMEM((coarse, width_mid), F32)],
        specs={4: carried_stat},
        near=(0, 1, 3, 4, 5, 6, 7, 8, 9, 10),
    )
    all_two_back = exchanged(stat_two_back)
    grad_expand, grad_short, back_short = run(
        wide_grads_kernel,
        [
            far((width_mid, width_in), BF16),
            far((width_in, width_in), BF16),
            far((coarse, width_in), BF16),
        ],
        (act_two, dconv_three, sub_in, dconv_short, w_short),
    )
    dconv_two, back_local, going, sums_one, stat_one_back = run(
        functools.partial(back_one_kernel, members_mid),
        [far((coarse, width_mid), BF16), far((fine, width_mid), F32), rims, sum_mid, stat],
        (
            back_two,
            conv_two,
            vec_two,
            all_two_back,
            gains_mid,
            shifts_mid,
            w_spatial,
            conv_one,
            prior_rims,
            vec_one,
            links_across,
        ),
        [
            pltpu.VMEM((9, QUARTER, tiles, width_mid), F32),
            pltpu.VMEM((2 * SIDE, tiles, width_mid), F32),
        ],
        near=(0, 1, 2, 3, 4, 5, 6, 9, 10),
    )
    all_one_back = exchanged(stat_one_back)
    from_next = lax.ppermute(going, "space", [(i + 1, i) for i in range(spaces - 1)])
    share_spatial = 9 * width_mid // spaces
    halves = [make((spaces, HALF_ROWS, LANES), BF16) for make in (far, struct)]
    keep, send = run(
        mid_grads_kernel,
        halves,
        (core, columns, dconv_two, grad_expand, grad_short, sums_wide, sums_two, sums_one),
        [
            pltpu.VMEM((9 * width_mid, width_mid), F32),
            pltpu.VMEM((spaces, 48, LANES), F32),
            pltpu.VMEM((spaces, 2 * HALF_ROWS, LANES), BF16),
        ],
        (0,),
    )
    twin = lax.ppermute(send, "dp", [(i, i ^ 1) for i in range(dps)])
    dconv_one, outbound = run(
        functools.partial(first_grad_kernel, members_in),
        [far((fine, width_mid), BF16), struct((spaces, SUM_ROWS, LANES), BF16)],
        (back_local, conv_one, from_next, vec_one, all_one_back, gains_mid, shifts_mid, flat_in, keep, twin),
        [pltpu.VMEM((fine, width_mid), F32)],
        near=(2, 3, 4, 5, 6, 9),
    )
    inbound = exchanged(outbound)
    grad_features = pl.pallas_call(
        features_kernel,
        name="featgrad",
        compiler_params=small_grant(),
        grid=(4,),
        in_specs=[
            pl.BlockSpec((fine // 4, width_mid), lambda g: (g, 0)),
            pl.BlockSpec((width_in, width_mid), lambda g: (0, 0)),
            pl.BlockSpec((coarse // 4, width_in), lambda g: (g, 0)),
        ],
        out_specs=pl.BlockSpec((fine // 4, width_in), lambda g: (g, 0)),
        out_shape=far((fine, width_in), BF16),
    )(held(dconv_one), held(w_reduce), held(back_short))
    (mine,) = run(total_kernel, [struct((dps, SUM_ROWS, LANES), BF16)], (inbound,), near=(0,))
    everyone = exchanged(mine, "dp")
    scale_in = 1.0 / math.sqrt(slide_count * tiles_total * POSITIONS)
    scale_out = 1.0 / math.sqrt(slide_count * tiles_total * QUARTER)
    shares = run(
        functools.partial(final_kernel, scale_in, scale_out),
        [
            far((width_in // spaces, width_mid), F32),
            far((share_spatial, width_mid), F32),
            far((width_mid // spaces, width_in), F32),
            far((width_in // spaces, width_in), F32),
            far((2, width_mid // spaces), F32),
            far((2, width_mid // spaces), F32),
            far((2, width_in // spaces), F32),
            far((2, width_in // spaces), F32),
        ],
        (everyone,),
        [pltpu.VMEM((144, LANES), F32)],
        near=(0,),
    )
    return (
        block_out[None],
        grad_features.reshape(1, tiles, POSITIONS, width_in),
        *shares,
    )


def solution(mesh):
    placed = (
        P("dp", "space", None, None),
        P("dp", "space", None),
        P("dp", "space", None),
        P(),
        P(),
        P(),
        P(),
        P(),
        P(),
        P(),
        P(),
        P("dp", "space", None, None),
    )
    return jax.shard_map(
        step,
        mesh=mesh,
        in_specs=placed,
        out_specs=(
            P("dp", "space", None, None),
            P("dp", "space", None, None),
            P("space", None),
            P("space", None),
            P("space", None),
            P("space", None),
            P(None, "space"),
            P(None, "space"),
            P(None, "space"),
            P(None, "space"),
        ),
        check_vma=False,
    )
```

time: 1530 us -> 201 us (0.13)
  blocking collectives: 536 us -> 83.3 us
  local copies, waits for them, and re-layouts: 399 us -> 0.75 us
  waiting for transfers between devices: 429 us -> 35.3 us
  other arithmetic: 43.4 us -> 0.01 us
  Pallas kernels: 0 us -> 42.6 us
  starting transfers between devices: 69.4 us -> 36.1 us
  matrix products: 25.9 us -> 0 us
  between operations: 17.1 us -> 0.8 us
    psum x7 -> x0, blocking collectives: 462 us -> none  [the longest x6 437 us: slide_total(): return lax.psum(partial_sums, 'space')]
    unnamed x14 -> x0, waiting for transfers between devices: 424 us -> none
    slice x26 -> x0, local copies, waits for them, and re-layouts: 330 us -> none  [the longest x9 269 us: body(): padded[:, offset_row:offset_row + SIDE - 1:2, offset_col:offset_col + SID...]
    all_to_all x0 -> x4, blocking collectives: none -> 83.3 us  [exchanged(): return lax.all_to_all(array, axis, 0, 0, tiled=True)]
    unnamed x1 -> x0, blocking collectives: 73.4 us -> none
    unnamed x11 -> x0, starting transfers between devices: 45.8 us -> none
    pallas_call x0 -> x14, Pallas kernels: none -> 42.6 us  [the longest x11 30.4 us: run(): pl.pallas_call(kernel, grid=(1,), out_shape=outs, in_specs=in_specs, out_...]
    all_to_all x2 -> x4, waiting for transfers between devices: 0.01 us -> 29.9 us  [exchanged(): return lax.all_to_all(array, axis, 0, 0, tiled=True)]
  transfers between devices with their start and end apart: 15 -> 7, of which waited for: 5 -> 5; matrix products, arithmetic and copies ran while one was open for 29% -> 0% of each run, Pallas kernels for 0% -> 6%
where the time goes in v1:
time: 201 us; the launch traced here: 199 us
  blocking collectives  83.3 us (41%)
  Pallas kernels  42.6 us (21%)
  starting transfers between devices  36.1 us (18%)
  waiting for transfers between devices  35.3 us (18%)
    all_to_all x4, blocking collectives, exchanged(): return lax.all_to_all(array, axis, 0, 0, tiled=True)  83.3 us
    pallas_call x11, Pallas kernels, run(): pl.pallas_call(kernel, grid=(1,), out_shape=outs, in_specs=in_specs, out_...  30.4 us
    all_to_all x4, waiting for transfers between devices, exchanged(): return lax.all_to_all(array, axis, 0, 0, tiled=True)  29.9 us
    all_to_all x4, starting transfers between devices, exchanged(): return lax.all_to_all(array, axis, 0, 0, tiled=True)  29.7 us
    ppermute x1, waiting for transfers between devices, step(): lax.ppermute(own_rims, 'space', [(i, i + 1) for i in range(spaces - 1)])  5.34 us
    pallas_call x1, Pallas kernels, step(): pl.pallas_call(features_kernel, name='featgrad', compiler_params=small_gr...  4.48 us
    pallas_call x1, Pallas kernels, step(): pl.pallas_call(reduce_kernel, name='reduce', compiler_params=small_grant(...  4.46 us
  transfers between devices with their start and end apart: 7, of which 5 were waited for; matrix products, arithmetic and copies ran while one was open for 0% of the time, Pallas kernels for 6%

profile of v1, /device:TPU:4, one launch (start us, length us, event | category | flops | bytes accessed | tf_op | source)
XLA Modules:
  0.0 198.8 jit_solution(5963842218221521822)
XLA Ops:
  0.6 4.5 %reduce.1 = (bf16[64,32,128]{2,1,0:T(8,128)(2,1)}, bf16[16,32,128]{2,1,0:T(8,128)(2,1)S(1)}, bf16[32,136,128]{2,1,0:T(8,128)(2,1)}) custom-call(bf16[2048,512]{1,0:T(8,128)(2,1)} %bitcast.13, bf16[512,128]{1,0:T(8,128)(2,1)} %w_ref.15, bf16[32,32,512]{2,1,0:T(8,128)(2,1)} %bitcast.17), custom_call_target="tpu_custom_call" | custom-call | tf_op jit(solution)/shard_map/reduce/pallas_call | solution.py:720
  5.1 0.0 copy-start.9
  5.1 0.0 copy-start.1
  5.1 0.0 copy-start.4
  5.1 0.0 copy-start.5
  5.1 11.7 %all-to-all-start = ((bf16[32,136,128]{2,1,0:T(8,128)(2,1)}), bf16[32,136,128]{2,1,0:T(8,128)(2,1)S(1)}, u32[]{:S(2)}, u32[]{:S(2)}) async-start(bf16[32,136,128]{2,1,0:T(8,128)(2,1)} %get-tuple-element.55), calls=%async_computation | async-start | bytes 2228224 | tf_op jit(solution)/shard_map/all_to_all | solution.py:709
  16.9 3.1 %collective-permute-start = (bf16[16,32,128]{2,1,0:T(8,128)(2,1)S(1)}, bf16[16,32,128]{2,1,0:T(8,128)(2,1)S(1)}, u32[]{:S(2)}, u32[]{:S(2)}) collective-permute-start(bf16[16,32,128]{2,1,0:T(8,128)(2,1)S(1)} %get-tuple-element.54), channel_id=1, source_target_pairs={{0,1},{1,2},{2,3},{3,4},{4,5},{5,6},{6,7},{7,8},{8,9},{9,10},{10,1... | collective-permute-start | bytes 393224 | tf_op jit(solution)/shard_map/ppermute | solution.py:739
  20.0 0.0 copy-done.9
  20.0 0.7 copy.22.link_ref
  20.7 5.3 %collective-permute-done.prior_ref = bf16[16,32,128]{2,1,0:T(8,128)(2,1)S(1)} collective-permute-done((bf16[16,32,128]{2,1,0:T(8,128)(2,1)S(1)}, bf16[16,32,128]{2,1,0:T(8,128)(2,1)S(1)}, u32[]{:S(2)}, u32[]{:S(2)}) %collective-permute-start) | collective-permute-done | bytes 131104 | tf_op jit(solution)/shard_map/ppermute | solution.py:739
  26.0 0.0 copy-start.3
  26.0 20.3 %all-to-all-done.g_ref.cot_ref = bf16[32,136,128]{2,1,0:T(8,128)(2,1)S(1)} async-done(((bf16[32,136,128]{2,1,0:T(8,128)(2,1)}), bf16[32,136,128]{2,1,0:T(8,128)(2,1)S(1)}, u32[]{:S(2)}, u32[]{:S(2)}) %all-to-all-start) | async-done | bytes 1114144 | tf_op jit(solution)/shard_map/all_to_all | solution.py:709
  46.3 0.0 copy-start
  46.3 0.0 copy-done.1
  46.3 0.0 copy-done.4
  46.4 0.0 copy-done.5
  46.4 3.8 %shard_map.195 = (bf16[512,128]{1,0:T(8,128)(2,1)S(1)}, bf16[512,1152]{1,0:T(8,128)(2,1)}, f32[8,128]{1,0:T(8,128)S(1)}, f32[32,1,128]{2,1,0:T(1,128)}) custom-call(bf16[64,32,128]{2,1,0:T(8,128)(2,1)} %get-tuple-element.53.c1_ref, bf16[16,32,128]{2,1,0:T(8,128)(2,1)S(1)} %collective-permute-done.prior_ref, ...), custom_call_target="tpu_custom_call" | custom-call | tf_op jit(solution)/shard_map/pallas_call | solution.py:54
  50.1 7.5 %all-to-all-start.1 = ((f32[32,1,128]{2,1,0:T(1,128)}), f32[32,1,128]{2,1,0:T(1,128)S(1)}, u32[]{:S(2)}, u32[]{:S(2)}) async-start(f32[32,1,128]{2,1,0:T(1,128)} %get-tuple-element.57), calls=%async_computation.1 | async-start | bytes 32768 | tf_op jit(solution)/shard_map/all_to_all | solution.py:709
  57.6 0.0 copy-start.2
  57.6 0.0 copy-start.6
  57.6 0.0 copy-start.7
  57.7 0.0 copy-start.8
  57.7 3.2 %short.1 = (bf16[512,512]{1,0:T(8,128)(2,1)}, bf16[512,512]{1,0:T(8,128)(2,1)S(1)}, f32[8,512]{1,0:T(8,128)S(1)}) custom-call(bf16[2048,512]{1,0:T(8,128)(2,1)} %bitcast.14, bf16[512,512]{1,0:T(8,128)(2,1)} %w_ref.14), custom_call_target="tpu_custom_call" | custom-call | tf_op jit(solution)/shard_map/short/pallas_call | solution.py:740
  60.9 0.0 copy-done.3
  60.9 0.0 copy-done
  60.9 4.3 %all-to-all-done.1.g_ref = f32[32,1,128]{2,1,0:T(1,128)S(1)} async-done(((f32[32,1,128]{2,1,0:T(1,128)}), f32[32,1,128]{2,1,0:T(1,128)S(1)}, u32[]{:S(2)}, u32[]{:S(2)}) %all-to-all-start.1) | async-done | bytes 16416 | tf_op jit(solution)/shard_map/all_to_all | solution.py:709
  65.2 0.0 copy-done.2
  65.2 1.5 shard_map.196
  66.8 12.9 %all_to_all.40.g_ref = f32[32,1,128]{2,1,0:T(1,128)S(1)} all-to-all(f32[32,1,128]{2,1,0:T(1,128)S(1)} %get-tuple-element.61), channel_id=1, replica_groups=mesh['dp'=8,'space'=32] {'space'}, dimensions={0} | all-to-all | bytes 32768 | tf_op jit(solution)/shard_map/all_to_all | solution.py:709
  79.7 0.0 copy-done.6
  79.7 0.0 copy-done.7
  79.7 0.0 copy-done.8
  79.7 4.6 %shard_map.197 = (bf16[32,136,128]{2,1,0:T(8,128)(2,1)S(1)}, f32[512,512]{1,0:T(8,128)}, f32[8,512]{1,0:T(8,128)S(1)}, f32[8,512]{1,0:T(8,128)}) custom-call(s32[32]{0:T(128)S(1)} %bitcast.12, bf16[512,512]{1,0:T(8,128)(2,1)S(1)} %get-tuple-element.59.c3_ref, bf16[512,512]{1,0:T(8,128)(2,1)S(1)} %get-tuple-element.60.cs_ref, ...), custom_call_target="tpu_custom_call" | custom-call | tf_op jit(solution)/shard_map/pallas_call | solution.py:54
  84.3 32.7 %all_to_all.41.in_ref.g_ref = bf16[32,136,128]{2,1,0:T(8,128)(2,1)S(1)} all-to-all(bf16[32,136,128]{2,1,0:T(8,128)(2,1)S(1)} %get-tuple-element.62), channel_id=1, replica_groups=mesh['dp'=8,'space'=32] {'space'}, dimensions={0} | all-to-all | bytes 2228224 | tf_op jit(solution)/shard_map/all_to_all | solution.py:709
  117.0 3.5 %shard_map.199 = (bf16[512,512]{1,0:T(8,128)(2,1)}, bf16[512,512]{1,0:T(8,128)(2,1)}, f32[512,128]{1,0:T(8,128)S(1)}, f32[8,128]{1,0:T(8,128)}, f32[32,1,128]{2,1,0:T(1,128)}) custom-call(bf16[512,512]{1,0:T(8,128)(2,1)S(1)} %get-tuple-element.59.c3_ref, bf16[512,512]{1,0:T(8,128)(2,1)S(1)} %get-tuple-element.60.cs_ref, ...), custom_call_target="tpu_custom_call" | custom-call | tf_op jit(solution)/shard_map/pallas_call | solution.py:54
  120.5 6.0 %all-to-all-start.4 = ((f32[32,1,128]{2,1,0:T(1,128)}), f32[32,1,128]{2,1,0:T(1,128)S(1)}, u32[]{:S(2)}, u32[]{:S(2)}) async-start(f32[32,1,128]{2,1,0:T(1,128)} %get-tuple-element.67), calls=%async_computation.4 | async-start | bytes 32768 | tf_op jit(solution)/shard_map/all_to_all | solution.py:709
  126.5 3.2 %shard_map.201 = (bf16[128,512]{1,0:T(8,128)(2,1)}, bf16[512,512]{1,0:T(8,128)(2,1)}, bf16[512,512]{1,0:T(8,128)(2,1)}) custom-call(bf16[512,128]{1,0:T(8,128)(2,1)} %get-tuple-element.74.act_ref, bf16[512,512]{1,0:T(8,128)(2,1)} %get-tuple-element.75.d3_ref, bf16[512,512]{1,0:T(8,128)(2,1)} %get-tuple-element.76.sub_ref, ...), custom_call_target="tpu_custom_call" | custom-call | tf_op jit(solution)/shard_map/pallas_call | solution.py:54
  129.7 4.5 %all-to-all-done.4.g_ref = f32[32,1,128]{2,1,0:T(1,128)S(1)} async-done(((f32[32,1,128]{2,1,0:T(1,128)}), f32[32,1,128]{2,1,0:T(1,128)S(1)}, u32[]{:S(2)}, u32[]{:S(2)}) %all-to-all-start.4) | async-done | bytes 16416 | tf_op jit(solution)/shard_map/all_to_all | solution.py:709
  134.2 3.4 %shard_map.200 = (bf16[512,128]{1,0:T(8,128)(2,1)}, f32[2048,128]{1,0:T(8,128)}, bf16[16,32,128]{2,1,0:T(8,128)(2,1)S(1)}, f32[8,128]{1,0:T(8,128)}, f32[32,1,128]{2,1,0:T(1,128)S(1)}) custom-call(f32[512,128]{1,0:T(8,128)S(1)} %get-tuple-element.66.b2_ref, bf16[512,128]{1,0:T(8,128)(2,1)S(1)} %get-tuple-element.56.c2_ref, ...), custom_call_target="tpu_custom_call" | custom-call | tf_op jit(solution)/shard_map/pallas_call | solution.py:54
  137.7 3.1 %shard_map.202 = (bf16[32,64,128]{2,1,0:T(8,128)(2,1)}, bf16[32,64,128]{2,1,0:T(8,128)(2,1)S(1)}) custom-call(s32[1]{0:T(128)} %bitcast.5.core_ref, bf16[512,1152]{1,0:T(8,128)(2,1)} %get-tuple-element.72.col_ref, bf16[512,128]{1,0:T(8,128)(2,1)} %get-tuple-element.73.d2_ref, bf16[128,512]{1,0:T(8,128)(2,1)} %get-tuple-element.78.ge_ref, ...), custom_call_target="tpu_custom_call" | custom-call | tf_op jit(solution)/shard_map/pallas_call | solution.py:54
  140.8 0.0 collective-permute-start.2
  140.8 3.3 %collective-permute-start.1 = (bf16[16,32,128]{2,1,0:T(8,128)(2,1)S(1)}, bf16[16,32,128]{2,1,0:T(8,128)(2,1)S(1)}, u32[]{:S(2)}, u32[]{:S(2)}) collective-permute-start(bf16[16,32,128]{2,1,0:T(8,128)(2,1)S(1)} %get-tuple-element.70), channel_id=1, source_target_pairs={{1,0},{2,1},{3,2},{4,3},{5,4},{6,5},{7,6},{8,7},{9,8},{10,9},{11,1... | collective-permute-start | bytes 393224 | tf_op jit(solution)/shard_map/ppermute | solution.py:858
  144.1 13.8 %all_to_all.42.g_ref = f32[32,1,128]{2,1,0:T(1,128)S(1)} all-to-all(f32[32,1,128]{2,1,0:T(1,128)S(1)} %get-tuple-element.71), channel_id=1, replica_groups=mesh['dp'=8,'space'=32] {'space'}, dimensions={0} | all-to-all | bytes 32768 | tf_op jit(solution)/shard_map/all_to_all | solution.py:709
  157.9 0.0 collective-permute-done.1.rim_ref
  157.9 0.0 collective-permute-done.2.twin_ref
  157.9 4.5 %shard_map.203 = (bf16[2048,128]{1,0:T(8,128)(2,1)}, bf16[32,80,128]{2,1,0:T(8,128)(2,1)S(1)}) custom-call(f32[2048,128]{1,0:T(8,128)} %get-tuple-element.69.b1_ref, bf16[64,32,128]{2,1,0:T(8,128)(2,1)} %get-tuple-element.53.c1_ref, bf16[16,32,128]{2,1,0:T(8,128)(2,1)S(1)} %collective-permute-done.1.rim_ref, f32[8,128]{1,0:T(8,128)S(1)} %get-tuple-element.68.v1_ref, ...), custom_call_target="tpu_custom_call" | custom-call | tf_op jit(solution)/shard_map/pallas_call | solution.py:54
  162.4 23.9 %all_to_all.43.in_ref = bf16[32,80,128]{2,1,0:T(8,128)(2,1)S(1)} all-to-all(bf16[32,80,128]{2,1,0:T(8,128)(2,1)S(1)} %get-tuple-element.87), channel_id=1, replica_groups=mesh['dp'=8,'space'=32] {'space'}, dimensions={0} | all-to-all | bytes 1310720 | tf_op jit(solution)/shard_map/all_to_all | solution.py:709
  186.3 0.8 shard_map.204
  187.1 4.5 %all-to-all-start.7 = ((bf16[8,80,128]{2,1,0:T(8,128)(2,1)}), bf16[8,80,128]{2,1,0:T(8,128)(2,1)S(1)}, u32[]{:S(2)}, u32[]{:S(2)}) async-start(bf16[8,80,128]{2,1,0:T(8,128)(2,1)} %shard_map.204), calls=%async_computation.7 | async-start | bytes 327680 | tf_op jit(solution)/shard_map/all_to_all | solution.py:709
  191.6 1.2 shard_map.198
  192.8 4.5 %featgrad.1 = bf16[2048,512]{1,0:T(8,128)(2,1)} custom-call(bf16[2048,128]{1,0:T(8,128)(2,1)} %get-tuple-element.85.d1_ref, bf16[512,128]{1,0:T(8,128)(2,1)} %w_ref.15, bf16[512,512]{1,0:T(8,128)(2,1)} %get-tuple-element.86.bs_ref), custom_call_target="tpu_custom_call" | custom-call | tf_op jit(solution)/shard_map/featgrad/pallas_call | solution.py:881
  197.2 0.8 all-to-all-done.7.in_ref
  198.0 0.8 shard_map.205
  (3 shorter events, 0.0 us)
Async XLA Ops:
  5.1 14.9 %copy-start.9 = (s32[1,32,3]{1,0,2:T(1,128)S(1)}, s32[1,32,3]{1,0,2:T(1,128)}, u32[]{:S(2)}) copy-start(s32[1,32,3]{1,0,2:T(1,128)} %param.14) | copy-start | bytes 1156
  5.1 41.2 %copy-start.1 = (bf16[1152,128]{1,0:T(8,128)(2,1)S(1)}, bf16[1152,128]{1,0:T(8,128)(2,1)}, u32[]{:S(2)}) copy-start(bf16[1152,128]{1,0:T(8,128)(2,1)} %w_ref.13) | copy-start | bytes 884740
  5.1 41.2 %copy-start.4 = (f32[2,128]{1,0:T(2,128)S(1)}, f32[2,128]{1,0:T(2,128)}, u32[]{:S(2)}) copy-start(f32[2,128]{1,0:T(2,128)} %gain_ref.11) | copy-start | bytes 3076
  5.1 41.2 %copy-start.5 = (f32[2,128]{1,0:T(2,128)S(1)}, f32[2,128]{1,0:T(2,128)}, u32[]{:S(2)}) copy-start(f32[2,128]{1,0:T(2,128)} %shift_ref.9) | copy-start | bytes 3076
  5.1 41.2 %all-to-all-start = ((bf16[32,136,128]{2,1,0:T(8,128)(2,1)}), bf16[32,136,128]{2,1,0:T(8,128)(2,1)S(1)}, u32[]{:S(2)}, u32[]{:S(2)}) async-start(bf16[32,136,128]{2,1,0:T(8,128)(2,1)} %get-tuple-element.55), calls=%async_computation | async-start | bytes 2228224 | tf_op jit(solution)/shard_map/all_to_all | solution.py:709
  16.9 9.2 %collective-permute-start = (bf16[16,32,128]{2,1,0:T(8,128)(2,1)S(1)}, bf16[16,32,128]{2,1,0:T(8,128)(2,1)S(1)}, u32[]{:S(2)}, u32[]{:S(2)}) collective-permute-start(bf16[16,32,128]{2,1,0:T(8,128)(2,1)S(1)} %get-tuple-element.54), channel_id=1, source_target_pairs={{0,1},{1,2},{2,3},{3,4},{4,5},{5,6},{6,7},{7,8},{8,9},{9,10},{10,1... | collective-permute-start | bytes 393224 | tf_op jit(solution)/shard_map/ppermute | solution.py:739
  26.0 34.9 %copy-start.3 = (bf16[16,32,128]{2,1,0:T(8,128)(2,1)}, bf16[16,32,128]{2,1,0:T(8,128)(2,1)S(1)}, u32[]{:S(2)}) copy-start(bf16[16,32,128]{2,1,0:T(8,128)(2,1)S(1)} %collective-permute-done.prior_ref) | copy-start | bytes 393220
  46.3 14.5 %copy-start = (bf16[32,136,128]{2,1,0:T(8,128)(2,1)}, bf16[32,136,128]{2,1,0:T(8,128)(2,1)S(1)}, u32[]{:S(2)}) copy-start(bf16[32,136,128]{2,1,0:T(8,128)(2,1)S(1)} %all-to-all-done.g_ref.cot_ref) | copy-start | bytes 3342340
  50.1 15.1 %all-to-all-start.1 = ((f32[32,1,128]{2,1,0:T(1,128)}), f32[32,1,128]{2,1,0:T(1,128)S(1)}, u32[]{:S(2)}, u32[]{:S(2)}) async-start(f32[32,1,128]{2,1,0:T(1,128)} %get-tuple-element.57), calls=%async_computation.1 | async-start | bytes 32768 | tf_op jit(solution)/shard_map/all_to_all | solution.py:709
  57.6 7.6 %copy-start.2 = (bf16[128,512]{1,0:T(8,128)(2,1)S(1)}, bf16[128,512]{1,0:T(8,128)(2,1)}, u32[]{:S(2)}) copy-start(bf16[128,512]{1,0:T(8,128)(2,1)} %w_ref.12) | copy-start | bytes 393220
  57.6 22.1 %copy-start.6 = (f32[2,512]{1,0:T(2,128)S(1)}, f32[2,512]{1,0:T(2,128)}, u32[]{:S(2)}) copy-start(f32[2,512]{1,0:T(2,128)} %gain_ref.9) | copy-start | bytes 12292
  57.6 22.0 %copy-start.7 = (f32[2,512]{1,0:T(2,128)S(1)}, f32[2,512]{1,0:T(2,128)}, u32[]{:S(2)}) copy-start(f32[2,512]{1,0:T(2,128)} %shift_ref.7) | copy-start | bytes 12292
  57.7 22.0 %copy-start.8 = (s32[1,32,1]{1,2,0:T(1,128)S(1)}, s32[1,32,1]{1,2,0:T(1,128)}, u32[]{:S(2)}) copy-start(s32[1,32,1]{1,2,0:T(1,128)} %param.13) | copy-start | bytes 388
  120.5 13.7 %all-to-all-start.4 = ((f32[32,1,128]{2,1,0:T(1,128)}), f32[32,1,128]{2,1,0:T(1,128)S(1)}, u32[]{:S(2)}, u32[]{:S(2)}) async-start(f32[32,1,128]{2,1,0:T(1,128)} %get-tuple-element.67), calls=%async_computation.4 | async-start | bytes 32768 | tf_op jit(solution)/shard_map/all_to_all | solution.py:709
  140.8 17.1 %collective-permute-start.2 = (bf16[32,64,128]{2,1,0:T(8,128)(2,1)S(1)}, bf16[32,64,128]{2,1,0:T(8,128)(2,1)S(1)}, u32[]{:S(2)}, u32[]{:S(2)}) collective-permute-start(bf16[32,64,128]{2,1,0:T(8,128)(2,1)S(1)} %get-tuple-element.84), channel_id=1, source_target_pairs={{0,32},{32,0},{64,96},{96,64},{128,160},{160,128},{192,224},{224,1... | collective-permute-start | bytes 1572872 | tf_op jit(solution)/shard_map/ppermute | solution.py:872
  140.8 17.1 %collective-permute-start.1 = (bf16[16,32,128]{2,1,0:T(8,128)(2,1)S(1)}, bf16[16,32,128]{2,1,0:T(8,128)(2,1)S(1)}, u32[]{:S(2)}, u32[]{:S(2)}) collective-permute-start(bf16[16,32,128]{2,1,0:T(8,128)(2,1)S(1)} %get-tuple-element.70), channel_id=1, source_target_pairs={{1,0},{2,1},{3,2},{4,3},{5,4},{6,5},{7,6},{8,7},{9,8},{10,9},{11,1... | collective-permute-start | bytes 393224 | tf_op jit(solution)/shard_map/ppermute | solution.py:858
  187.1 10.9 %all-to-all-start.7 = ((bf16[8,80,128]{2,1,0:T(8,128)(2,1)}), bf16[8,80,128]{2,1,0:T(8,128)(2,1)S(1)}, u32[]{:S(2)}, u32[]{:S(2)}) async-start(bf16[8,80,128]{2,1,0:T(8,128)(2,1)} %shard_map.204), calls=%async_computation.7 | async-start | bytes 327680 | tf_op jit(solution)/shard_map/all_to_all | solution.py:709
